TPU v7x, 32 devices: a whole 2x2x4 slice. The times are simulated.
32 devices in a mesh: dp: 8 (over z, x), tensor: 4 (over y, core).
Axes of the slice: x: 2, y: 2, z: 4, core: 2. Of those that a mesh axis runs over, the one named last changes fastest.
Arguments:
- tokens: bfloat16 [4096, 768], P(('dp', 'tensor')), may hold values from -6 to 6
- attn_gain: bfloat16 [768], P('dp'), may hold values from 0.25 to 1.75
- w_qkv: bfloat16 [3, 768, 768], P(None, 'dp', 'tensor'), may hold values from -14.072913 to 14.072913
- w_out: bfloat16 [768, 768], P('tensor', 'dp'), may hold values from -3 to 3
- mlp_gain: bfloat16 [768], P('dp'), may hold values from 0.25 to 1.75
- w_in: bfloat16 [2, 768, 1152], P(None, 'dp', 'tensor'), may hold values from -0.21875 to 0.21875
- w_down: bfloat16 [1152, 768], P('tensor', 'dp'), may hold values from -0.1875 to 0.1875
- cotangent: bfloat16 [4096, 768], P(('dp', 'tensor')), may hold values from -6 to 6
Outputs:
- out: bfloat16 [4096, 768], P(('dp', 'tensor'))
- input_grad: float32 [4096, 768], P(('dp', 'tensor'))
- attn_gain_grad: float32 [768], P('dp')
- w_qkv_grad: float32 [3, 768, 768], P(None, 'dp', 'tensor')
- w_out_grad: float32 [768, 768], P('tensor', 'dp')
- mlp_gain_grad: float32 [768], P('dp')
- w_in_grad: float32 [2, 768, 1152], P(None, 'dp', 'tensor')
- w_down_grad: float32 [1152, 768], P('tensor', 'dp')
All inputs are finite; a program needn't handle non-finite values.
Results may differ from a plain program's by a relative error of at most 0.013.
Values may be sent and summed in bfloat16 or wider, within the bound.
A program may use at most 64 MiB of HBM per device.

v0:
```python
import functools

import jax
import jax.numpy as jnp
from jax import lax
from jax.experimental import pallas as pl
from jax.experimental.pallas import tpu as pltpu
from jax.experimental.layout import Layout, with_layout_constraint
from jax.sharding import PartitionSpec as P

HD = 64
L = 512


NORM_EPS = 1e-05
ROPE_THETA = 160000.0
SQRT_HALF = 0.7071067811865476
GAUSS_NORM = 0.3989422804014327


def rope_tables(row_count):
    position = (jnp.arange(row_count) % L).astype(jnp.float32)
    halves = jnp.arange(HD // 2).astype(jnp.float32)
    inverse = ROPE_THETA ** (-2.0 * halves / HD)
    angles = position[:, None] * inverse[None, :]
    angles = jnp.concatenate([angles, angles], axis=1)
    return (jnp.cos(angles)[:, None, :], jnp.sin(angles)[:, None, :])


def rotate(field_rows, cos_table, sin_table):
    first_half = field_rows[..., : HD // 2]
    second_half = field_rows[..., HD // 2 :]
    turned = jnp.concatenate([-second_half, first_half], axis=-1)
    return field_rows * cos_table + turned * sin_table


def rotate_back(grad_field, cos_table, sin_table):
    scaled = grad_field * sin_table
    turned = jnp.concatenate([scaled[..., HD // 2 :], -scaled[..., : HD // 2]], axis=-1)
    return grad_field * cos_table + turned


def normalize(values):
    centred = values - jnp.mean(values, axis=-1, keepdims=True)
    inv_std = lax.rsqrt(jnp.mean(centred * centred, axis=-1, keepdims=True) + NORM_EPS)
    return (centred * inv_std, inv_std)


def normalize_back(grad_norm, normed, inv_std, gain_row):
    gain_part = jnp.sum(grad_norm * normed, axis=0)
    scaled = grad_norm * gain_row
    centred = scaled - jnp.mean(scaled, axis=-1, keepdims=True)
    grad_in = inv_std * (centred - normed * jnp.mean(scaled * normed, axis=-1, keepdims=True))
    return (grad_in, gain_part)


def gelu_pair(inputs):
    normal_cdf = 0.5 * (1.0 + lax.erf(inputs * SQRT_HALF))
    return (inputs * normal_cdf, normal_cdf + inputs * jnp.exp(-0.5 * inputs * inputs) * GAUSS_NORM)


def attend(queries, key_rows, value_rows):
    score_scale = HD ** (-0.5)
    scores = (
        jnp.einsum("qhd,khd->hqk", queries, key_rows, preferred_element_type=jnp.float32)
        * score_scale
    )
    row_max = jnp.max(scores, axis=-1, keepdims=True)
    log_total = row_max + jnp.log(jnp.sum(jnp.exp(scores - row_max), axis=-1, keepdims=True))
    weights = jnp.exp(scores - log_total).astype(jnp.bfloat16)
    attn_mix = jnp.einsum(
        "hqk,khd->qhd", weights, value_rows, preferred_element_type=jnp.float32
    ).astype(jnp.bfloat16)
    return (attn_mix, log_total)


def attend_back(queries, key_rows, value_rows, attn_mix, grad_mix, log_total):
    score_scale = HD ** (-0.5)
    scores = (
        jnp.einsum("qhd,khd->hqk", queries, key_rows, preferred_element_type=jnp.float32)
        * score_scale
    )
    probabilities = jnp.exp(scores - log_total)
    grad_probs = jnp.einsum(
        "qhd,khd->hqk", grad_mix, value_rows, preferred_element_type=jnp.float32
    )
    row_delta = jnp.sum(grad_mix.astype(jnp.float32) * attn_mix.astype(jnp.float32), axis=-1)
    grad_scores = (probabilities * (grad_probs - jnp.transpose(row_delta)[:, :, None])).astype(
        jnp.bfloat16
    )
    prob_rounded = probabilities.astype(jnp.bfloat16)
    grad_values = jnp.einsum(
        "hqk,qhd->khd", prob_rounded, grad_mix, preferred_element_type=jnp.float32
    )
    grad_queries = (
        jnp.einsum("hqk,khd->qhd", grad_scores, key_rows, preferred_element_type=jnp.float32)
        * score_scale
    )
    grad_keys = (
        jnp.einsum("hqk,qhd->khd", grad_scores, queries, preferred_element_type=jnp.float32)
        * score_scale
    )
    return (grad_queries, grad_keys, grad_values)


def exchange_kernel(plan, sizes, *refs):
    count = len(plan)
    sources, targets = refs[:count], refs[count : 2 * count]
    own_sem, send_sem, recv_sem = refs[2 * count :]
    axes = sorted({axis for _, axis, _ in plan})
    barrier = pltpu.get_barrier_semaphore()
    total = 0
    for axis in axes:
        me = lax.axis_index(axis)
        for shift in range(1, sizes[axis]):
            pl.semaphore_signal(
                barrier,
                inc=1,
                device_id={axis: lax.rem(me + shift, sizes[axis])},
                device_id_type=pl.DeviceIdType.MESH,
            )
            total += 1
    pl.semaphore_wait(barrier, total)
    slot = 0
    pending, relays, local = [], [], []

    def remote(source, target, axis, peer, index):
        return pltpu.make_async_remote_copy(
            src_ref=source,
            dst_ref=target,
            send_sem=send_sem.at[index],
            recv_sem=recv_sem.at[index],
            device_id={axis: peer},
            device_id_type=pl.DeviceIdType.MESH,
        )

    for which, (kind, axis, span) in enumerate(plan):
        size = sizes[axis]
        me = lax.axis_index(axis)
        source, target = sources[which], targets[which]
        outer = size // 2
        column = lax.rem(me, 2)
        row = me // 2
        partner = row * 2 + 1 - column
        if kind == "half":
            copy = remote(source.at[:, 1 - column, :, span], target, axis, partner, slot)
            copy.start()
            pending.append(copy)
            slot += 1
            continue
        if kind == "outer":
            for shift in range(1, outer):
                other = lax.rem(row + shift, outer)
                copy = remote(source.at[other], target.at[row], axis, other * 2 + column, slot)
                copy.start()
                pending.append(copy)
                slot += 1
            copy = pltpu.make_async_copy(source.at[row], target.at[row], own_sem.at[which])
            copy.start()
            local.append(copy)
            continue
        if kind == "relay":
            for shift in range(1, outer):
                peer = lax.rem(row + shift, outer) * 2 + column
                copy = remote(source, target.at[me], axis, peer, slot)
                copy.start()
                origin = lax.rem(row + outer - shift, outer) * 2 + column
                relays.append((copy, target, axis, origin, partner, slot + 1))
                slot += 2
            copy = remote(source, target.at[me], axis, partner, slot)
            copy.start()
            pending.append(copy)
            slot += 1
        else:
            for shift in range(1, size):
                peer = lax.rem(me + shift, size)
                piece = source if kind == "gather" else source.at[peer, :, span]
                copy = remote(piece, target.at[me], axis, peer, slot)
                copy.start()
                pending.append(copy)
                slot += 1
        piece = source if kind != "scatter" else source.at[me, :, span]
        copy = pltpu.make_async_copy(piece, target.at[me], own_sem.at[which])
        copy.start()
        local.append(copy)
    for copy, target, axis, origin, partner, index in relays:
        copy.wait_recv()
        onward = remote(target.at[origin], target.at[origin], axis, partner, index)
        onward.start()
        pending.append(onward)
    for copy, *_ in relays:
        copy.wait_send()
    for copy in pending + local:
        copy.wait()


def slots_of(kind, size):
    outer = size // 2
    return {"relay": 2 * outer - 1, "half": 1, "outer": outer - 1}.get(kind, size - 1)


def shape_of(kind, size, shape, wide):
    if kind == "half":
        return (shape[0], shape[2], wide)
    return {"scatter": shape[:-1] + (wide,), "outer": shape}.get(kind, (size,) + shape)


def exchange(sizes, number, *ops):
    arrays = [op[2] for op in ops]
    spans = [slice(*op[3]) if len(op) > 3 else slice(0, op[2].shape[-1]) for op in ops]
    plan = tuple((op[0], op[1], span) for op, span in zip(ops, spans))
    shapes = [
        jax.ShapeDtypeStruct(
            shape_of(kind, sizes[axis], array.shape, span.stop - span.start), array.dtype
        )
        for (kind, axis, span), array in zip(plan, arrays)
    ]
    slots = sum(slots_of(kind, sizes[axis]) for kind, axis, _ in plan)
    return pl.pallas_call(
        functools.partial(exchange_kernel, plan, sizes),
        out_shape=shapes,
        in_specs=[pl.BlockSpec(memory_space=pltpu.VMEM)] * len(arrays),
        out_specs=[pl.BlockSpec(memory_space=pltpu.VMEM)] * len(arrays),
        scratch_shapes=[
            pltpu.SemaphoreType.DMA((len(arrays),)),
            pltpu.SemaphoreType.DMA((slots,)),
            pltpu.SemaphoreType.DMA((slots,)),
        ],
        compiler_params=pltpu.CompilerParams(
            collective_id=number, has_side_effects=True, vmem_limit_bytes=48 << 20
        ),
    )(*arrays)


def pad_columns(array, multiple=128):
    extra = -array.shape[-1] % multiple
    return jnp.pad(array, [(0, 0)] * (array.ndim - 1) + [(0, extra)])


def total_of(pieces):
    return jnp.sum(pieces.astype(jnp.float32), axis=0)


def row_major(array):
    return with_layout_constraint(array, Layout(major_to_minor=(0, 1)))


def dot_f32(left, right, left_dim, right_dim):
    return lax.dot_general(
        left, right, (((left_dim,), (right_dim,)), ((), ())), preferred_element_type=jnp.float32
    )


def feed_forward_kernel(
    hidden, rows_ref, up_ref, gate_ref, down_ref, cot_ref, mlp_ref, back_ref, grads_ref
):
    bf16 = jnp.bfloat16
    rows, cot = rows_ref[...], cot_ref[...]
    inputs = dot_f32(rows, up_ref[...], 1, 0)
    gate_part = dot_f32(rows, gate_ref[...], 1, 0)
    activated, gelu_slope = gelu_pair(inputs)
    hidden_act = (activated * gate_part).astype(bf16)
    mlp_ref[...] = dot_f32(hidden_act, down_ref[...], 1, 1).astype(bf16)
    grad_act = dot_f32(cot, down_ref[...], 1, 0)
    grad_up = (grad_act * gate_part * gelu_slope).astype(bf16)
    grad_gate = (grad_act * activated).astype(bf16)
    back_ref[...] = (
        dot_f32(grad_up, up_ref[...], 1, 1) + dot_f32(grad_gate, gate_ref[...], 1, 1)
    ).astype(bf16)
    grads_ref[:, :hidden] = dot_f32(rows, grad_up, 0, 0).astype(bf16)
    grads_ref[:, hidden : 2 * hidden] = dot_f32(rows, grad_gate, 0, 0).astype(bf16)
    grads_ref[:, 2 * hidden : 3 * hidden] = dot_f32(cot, hidden_act, 0, 0).astype(bf16)
    spare = grads_ref.shape[1] - 3 * hidden
    if spare:
        grads_ref[:, 3 * hidden :] = jnp.zeros((grads_ref.shape[0], spare), bf16)


def feed_forward(hidden, rows, up, gate, down_t, cot):
    row_count, width = rows.shape
    padded = -(-3 * hidden // 128) * 128
    return pl.pallas_call(
        functools.partial(feed_forward_kernel, hidden),
        out_shape=[
            jax.ShapeDtypeStruct((row_count, width), jnp.bfloat16),
            jax.ShapeDtypeStruct((row_count, width), jnp.bfloat16),
            jax.ShapeDtypeStruct((width, padded), jnp.bfloat16),
        ],
        in_specs=[pl.BlockSpec(memory_space=pltpu.VMEM)] * 5,
        out_specs=[pl.BlockSpec(memory_space=pltpu.VMEM)] * 3,
        compiler_params=pltpu.CompilerParams(vmem_limit_bytes=48 << 20),
    )(rows, up, gate, down_t, cot)


def body(sizes, tokens, attn_gain, w_qkv, w_out, mlp_gain, w_in, w_down, cotangent):
    bf16, f32 = jnp.bfloat16, jnp.float32
    groups, members = sizes["dp"], sizes["tensor"]
    block = w_qkv.shape[1]
    width = block * groups
    heads_wide, hidden = w_qkv.shape[2], w_in.shape[2]
    own_rows = tokens.shape[0]
    packed = jnp.concatenate([w_qkv[0], w_qkv[1], w_qkv[2], w_out.T], axis=1)
    gain_tile = jnp.pad(jnp.stack([attn_gain, mlp_gain]), [(0, 14), (0, -block % 128)])
    weights, gain_tiles, token_rows, grad_rows = exchange(
        sizes,
        0,
        ("relay", "dp", packed),
        ("relay", "dp", gain_tile),
        ("relay", "tensor", tokens),
        ("relay", "tensor", cotangent),
    )
    weights = weights.reshape(width, -1)
    qkv_weight = weights[:, : 3 * heads_wide]
    out_weight_t = weights[:, 3 * heads_wide :]
    attn_full = gain_tiles[:, 0, :block].reshape(1, width).astype(f32)
    mlp_full = gain_tiles[:, 1, :block].reshape(1, width).astype(f32)
    outer = groups // 2
    column = lax.rem(lax.axis_index("dp"), 2)

    def quarter(array):
        return array.reshape(outer, 2, block, -1)

    def half_sum(array, received, low, high):
        own = lax.dynamic_index_in_dim(quarter(array)[..., low:high], column, 1, keepdims=False)
        return (own.astype(f32) + received.astype(f32)).astype(bf16)

    row_count = own_rows * members
    grad_rows = grad_rows.reshape(row_count, width)
    residual = tokens.astype(f32)
    normed_one, inv_one = normalize(residual)
    rows_one = (normalize(token_rows.reshape(row_count, width).astype(f32))[0] * attn_full).astype(bf16)
    head_count = heads_wide // HD
    head_shape = (row_count, head_count, HD)
    seq_shape = (row_count // L, L, head_count, HD)
    flat_shape = (row_count, heads_wide)
    cos_table, sin_table = rope_tables(row_count)
    projected = dot_f32(rows_one, qkv_weight, 1, 0)
    pieces = [projected[:, i * heads_wide : (i + 1) * heads_wide].reshape(head_shape) for i in range(3)]
    queries = rotate(pieces[0], cos_table, sin_table).astype(bf16).reshape(seq_shape)
    key_rows = rotate(pieces[1], cos_table, sin_table).astype(bf16).reshape(seq_shape)
    value_rows = pieces[2].astype(bf16).reshape(seq_shape)
    one_seq = row_count == L

    def over_sequences(function, arrays):
        if one_seq:
            results = function(*[array[0] for array in arrays])
            return tuple(result[None] for result in results)
        return lax.map(lambda seq_block: function(*seq_block), arrays)

    attn_mix, log_total = over_sequences(attend, (queries, key_rows, value_rows))
    mixed_rows = attn_mix.reshape(flat_shape)
    attn_part = dot_f32(mixed_rows, out_weight_t, 1, 1).astype(bf16)
    attn_parts, up_weight, down_weight_t = exchange(
        sizes,
        1,
        ("scatter", "tensor", attn_part.reshape(members, own_rows, width)),
        ("relay", "dp", w_in[0]),
        ("relay", "dp", w_down.T),
    )
    up_weight = up_weight.reshape(width, -1)
    down_weight_t = down_weight_t.reshape(width, -1)
    hidden_res = residual + total_of(attn_parts)
    normed_two, inv_two = normalize(hidden_res)
    ln_two = (normed_two * mlp_full).astype(bf16)
    rows_two, gate_weight = exchange(
        sizes, 2, ("relay", "tensor", ln_two), ("relay", "dp", w_in[1])
    )
    gate_weight = gate_weight.reshape(width, -1)
    rows_two = rows_two.reshape(row_count, width)
    mlp_part, ln_two_part, mlp_grads = feed_forward(
        hidden, rows_two, up_weight, gate_weight, down_weight_t, grad_rows
    )
    mlp_wide = mlp_grads.shape[-1]
    first = mlp_wide // 256 * 128
    ln_two_parts, mlp_grads_a = exchange(
        sizes,
        3,
        ("scatter", "tensor", ln_two_part.reshape(members, own_rows, width)),
        ("half", "dp", quarter(mlp_grads), (0, first)),
    )
    grad_res_two, mlp_gain_part = normalize_back(total_of(ln_two_parts), normed_two, inv_two, mlp_full)
    grad_hidden = cotangent.astype(f32) + grad_res_two
    grad_hidden_rows, mlp_grads_b, mlp_sums_a = exchange(
        sizes,
        4,
        ("relay", "tensor", grad_hidden.astype(bf16)),
        ("half", "dp", quarter(mlp_grads), (first, mlp_wide)),
        ("outer", "dp", half_sum(mlp_grads, mlp_grads_a, 0, first)),
    )
    grad_hidden_rows = grad_hidden_rows.reshape(row_count, width)
    grad_out_t = row_major(dot_f32(grad_hidden_rows, mixed_rows, 0, 0).astype(bf16))
    grad_mix = dot_f32(grad_hidden_rows, out_weight_t, 1, 0).astype(bf16).reshape(seq_shape)
    grad_q, grad_k, grad_v = over_sequences(
        attend_back, (queries, key_rows, value_rows, attn_mix, grad_mix, log_total)
    )
    grad_proj = jnp.concatenate(
        [
            rotate_back(grad_q.reshape(head_shape), cos_table, sin_table).reshape(flat_shape),
            rotate_back(grad_k.reshape(head_shape), cos_table, sin_table).reshape(flat_shape),
            grad_v.reshape(flat_shape),
        ],
        axis=1,
    ).astype(bf16)
    grad_qkv = row_major(dot_f32(rows_one, grad_proj, 0, 0).astype(bf16))
    ln_one_part = dot_f32(grad_proj, qkv_weight, 1, 1).astype(bf16)
    ln_one_parts, mlp_sums_b, grad_out_half, qkv_half = exchange(
        sizes,
        5,
        ("scatter", "tensor", ln_one_part.reshape(members, own_rows, width)),
        ("outer", "dp", half_sum(mlp_grads, mlp_grads_b, first, mlp_wide)),
        ("half", "dp", quarter(grad_out_t)),
        ("half", "dp", quarter(grad_qkv)),
    )
    grad_res_one, attn_gain_part = normalize_back(total_of(ln_one_parts), normed_one, inv_one, attn_full)
    input_grad = grad_hidden + grad_res_one
    gain_parts = jnp.stack([attn_gain_part, mlp_gain_part] + [jnp.zeros_like(attn_gain_part)] * 6)
    gain_parts = pad_columns(jnp.swapaxes(gain_parts.reshape(8, groups, block), 0, 1))
    late_parts, gain_parts, mlp_parts, grad_out_parts = exchange(
        sizes,
        6,
        ("outer", "dp", half_sum(grad_qkv, qkv_half, 0, 3 * heads_wide)),
        ("scatter", "dp", gain_parts),
        ("scatter", "tensor", mlp_part.reshape(members, own_rows, width)),
        ("outer", "dp", half_sum(grad_out_t, grad_out_half, 0, heads_wide)),
    )
    output = (hidden_res + total_of(mlp_parts)).astype(bf16)
    (gain_groups,) = exchange(sizes, 7, ("gather", "tensor", total_of(gain_parts)))
    gain_sum = total_of(gain_groups)
    late = total_of(late_parts)
    grad_w_qkv = jnp.stack([late[:, i * heads_wide : (i + 1) * heads_wide] for i in range(3)])
    grad_w_out = total_of(grad_out_parts).T
    mlp_sums = jnp.concatenate(
        [total_of(mlp_sums_a), total_of(mlp_sums_b)], axis=1
    )
    grad_w_in = jnp.stack([mlp_sums[:, :hidden], mlp_sums[:, hidden : 2 * hidden]])
    grad_w_down = mlp_sums[:, 2 * hidden : 3 * hidden].T
    return (
        output,
        input_grad,
        gain_sum[0, :block],
        grad_w_qkv,
        grad_w_out,
        gain_sum[1, :block],
        grad_w_in,
        grad_w_down,
    )


def solution(mesh):
    in_specs = (
        P(("dp", "tensor"), None),
        P("dp"),
        P(None, "dp", "tensor"),
        P("tensor", "dp"),
        P("dp"),
        P(None, "dp", "tensor"),
        P("tensor", "dp"),
        P(("dp", "tensor"), None),
    )
    out_specs = (
        P(("dp", "tensor"), None),
        P(("dp", "tensor"), None),
        P("dp"),
        P(None, "dp", "tensor"),
        P("tensor", "dp"),
        P("dp"),
        P(None, "dp", "tensor"),
        P("tensor", "dp"),
    )
    sizes = {axis: mesh.shape[axis] for axis in ("dp", "tensor")}
    return jax.shard_map(functools.partial(body, sizes), mesh=mesh, in_specs=in_specs, out_specs=out_specs, check_vma=False)
```

profile of v0, /device:TPU:0, one launch (start us, length us, event | category | flops | bytes accessed | tf_op | source)
XLA Modules:
  0.0 176.9 jit_solution(3795170534750988899)
XLA Ops:
  0.6 0.9 copy.42
  1.5 0.9 slice_bitcast_fusion.9
  3.2 0.9 copy-done.2
  4.1 0.9 copy-done.4
  5.0 24.9 %shard_map.143 = (bf16[8,96,768]{2,1,0:T(8,128)(2,1)S(1)}, bf16[8,16,128]{2,1,0:T(8,128)(2,1)S(1)}, bf16[4,128,768]{2,1,0:T(8,128)(2,1)S(1)}, bf16[4,128,768]{2,1,0:T(8,128)(2,1)S(1)}) custom-call(bf16[96,768]{1,0:T(8,128)(2,1)S(1)} %pad_maximum_fusion.6.refs_0_, bf16[16,128]{1,0:T(8,128)(2,1)S(1)} %fusion.40.refs_1_, bf16[128,768]{1,0:T(8,128)(2,1)S(1)} %copy-done.2, ...), custom_call_target="tpu_custom_call" | custom-call | tf_op jit(solution)/shard_map/pallas_call | solution.py:219
  32.6 1.0 broadcast_multiply_fusion.3
  35.1 1.1 copy-done.15
  38.9 0.9 copy-done.10
  39.8 0.9 copy-done.11
  40.7 21.4 %shard_map.144 = (bf16[4,128,768]{2,1,0:T(8,128)(2,1)S(1)}, bf16[8,96,288]{2,1,0:T(8,128)(2,1)S(1)}, bf16[8,96,288]{2,1,0:T(8,128)(2,1)S(1)}) custom-call(bf16[4,128,768]{2,1,0:T(8,128)(2,1)S(1)} %bitcast.117, bf16[96,288]{1,0:T(8,128)(2,1)S(1)} %copy-done.11, bf16[96,288]{1,0:T(8,128)(2,1)S(1)} %bitcast.136), custom_call_target="tpu_custom_call" | custom-call | tf_op jit(solution)/shard_map/pallas_call | solution.py:219
  63.1 1.3 fusion.51
  64.5 1.2 multiply_reduce_fusion.5
  65.7 1.1 multiply_convert_fusion.1.refs_0_
  66.8 15.6 %shard_map.145 = (bf16[4,128,768]{2,1,0:T(8,128)(2,1)S(1)}, bf16[8,96,288]{2,1,0:T(8,128)(2,1)S(1)}) custom-call(bf16[128,768]{1,0:T(8,128)(2,1)S(1)} %multiply_convert_fusion.1.refs_0_, bf16[96,288]{1,0:T(8,128)(2,1)S(1)} %copy-done.12), custom_call_target="tpu_custom_call" | custom-call | tf_op jit(solution)/shard_map/pallas_call | solution.py:219
  82.5 5.4 %shard_map.146 = (bf16[512,768]{1,0:T(8,128)(2,1)S(1)}, bf16[512,768]{1,0:T(8,128)(2,1)S(1)}, bf16[768,896]{1,0:T(8,128)(2,1)}) custom-call(bf16[512,768]{1,0:T(8,128)(2,1)S(1)} %bitcast.132, bf16[768,288]{1,0:T(8,128)(2,1)S(1)} %bitcast.133, bf16[768,288]{1,0:T(8,128)(2,1)S(1)} %bitcast.135, bf16[768,288]{1,0:T(8,128)(2,1)S(1)} %bitcast.134, ...), custom_call_target="tpu_custom_call" | custom-call | tf_op jit(solution)/shard_map/pallas_call | solution.py:281
  87.9 0.9 copy-done.6
  88.8 1.3 copy-done
  90.2 10.5 %shard_map.147 = (bf16[4,128,768]{2,1,0:T(8,128)(2,1)S(1)}, bf16[4,96,384]{2,1,0:T(8,128)(2,1)S(1)}) custom-call(bf16[4,128,768]{2,1,0:T(8,128)(2,1)S(1)} %bitcast.129, bf16[4,2,96,896]{3,2,1,0:T(8,128)(2,1)S(1)} %bitcast.113), custom_call_target="tpu_custom_call" | custom-call | tf_op jit(solution)/shard_map/pallas_call | solution.py:219
  101.6 0.9 fusion.50
  102.5 0.9 slice.130
  103.4 1.0 fusion.9.refs_2_
  104.5 14.6 %shard_map.148 = (bf16[4,128,768]{2,1,0:T(8,128)(2,1)S(1)}, bf16[4,96,512]{2,1,0:T(8,128)(2,1)S(1)}, bf16[4,96,384]{2,1,0:T(8,128)(2,1)S(1)}) custom-call(bf16[128,768]{1,0:T(8,128)(2,1)S(1)} %get-tuple-element.90.refs_0_, bf16[4,2,96,896]{3,2,1,0:T(8,128)(2,1)S(1)} %bitcast.115, bf16[4,96,384]{2,1,0:T(8,128)(2,1)S(1)} %fusion.9.refs_2_), custom_call_target="tpu_custom_call" | custom-call | tf_op jit(solution)/shard_map/pallas_call | solution.py:219
  120.7 0.9 multiply_convert_fusion
  123.1 0.8 copy-done.32
  124.1 0.8 convolution_convert_fusion.1
  126.2 0.8 convolution_convert_fusion
  127.0 18.5 %shard_map.149 = (bf16[4,128,768]{2,1,0:T(8,128)(2,1)S(1)}, bf16[4,96,512]{2,1,0:T(8,128)(2,1)S(1)}, bf16[4,96,192]{2,1,0:T(8,128)(2,1)S(1)}, bf16[4,96,576]{2,1,0:T(8,128)(2,1)S(1)}) custom-call(bf16[4,128,768]{2,1,0:T(8,128)(2,1)S(1)} %bitcast.131, bf16[4,96,512]{2,1,0:T(8,128)(2,1)S(1)} %fusion.8.refs_1_, bf16[4,2,96,192]{3,2,1,0:T(8,128)(2,1)S(1)} %bitcast.124, ...), custom_call_target="tpu_custom_call" | custom-call | tf_op jit(solution)/shard_map/pallas_call | solution.py:219
  146.5 0.9 add_rsqrt_fusion
  148.1 19.3 %shard_map.150 = (bf16[4,96,576]{2,1,0:T(8,128)(2,1)S(1)}, f32[8,8,128]{2,1,0:T(8,128)S(1)}, bf16[4,128,768]{2,1,0:T(8,128)(2,1)S(1)}, bf16[4,96,192]{2,1,0:T(8,128)(2,1)S(1)}) custom-call(bf16[4,96,576]{2,1,0:T(8,128)(2,1)S(1)} %fusion.4.refs_0_, f32[8,8,128]{2,1,0:T(8,128)S(1)} %pad.9.refs_1_, bf16[4,128,768]{2,1,0:T(8,128)(2,1)S(1)} %bitcast.128, ...), custom_call_target="tpu_custom_call" | custom-call | tf_op jit(solution)/shard_map/pallas_call | solution.py:219
  168.3 0.9 fusion.19
  169.3 3.7 %shard_map.151 = f32[4,8,128]{2,1,0:T(8,128)S(1)} custom-call(f32[8,128]{1,0:T(8,128)S(1)} %reduce_sum.234.refs_0_), custom_call_target="tpu_custom_call" | custom-call | tf_op jit(solution)/shard_map/pallas_call | solution.py:219
  176.2 0.8 copy.56
  (145 shorter events, 19.6 us)
Async XLA Ops:
  3.2 0.9 copy-start.2
  4.1 0.9 copy-start.4
  32.4 2.7 %copy-start.25 = (bf16[512,192]{0,1:T(8,128)(2,1)}, bf16[512,192]{0,1:T(8,128)(2,1)S(1)}, u32[]{:S(2)}) copy-start(bf16[512,192]{0,1:T(8,128)(2,1)S(1)} %slice.168) | copy-start | bytes 589828
  34.6 1.7 copy-start.15
  36.2 1.3 copy-start.34
  36.9 2.0 %copy-start.23 = (bf16[3,64,512]{2,1,0:T(8,128)(2,1)}, bf16[3,64,512]{2,1,0:T(8,128)(2,1)S(1)}, u32[]{:S(2)}) copy-start(bf16[3,64,512]{2,1,0:T(8,128)(2,1)S(1)} %convolution_convert_fusion.6) | copy-start | bytes 589828
  36.9 1.3 copy-start.35
  37.5 25.5 %copy-start.3 = (bf16[128,768]{1,0:T(8,128)(2,1)S(1)}, bf16[128,768]{1,0:T(8,128)(2,1)}, u32[]{:S(2)}) copy-start(bf16[128,768]{1,0:T(8,128)(2,1)} %refs_2_.1) | copy-start | bytes 589828
  62.1 2.3 %copy-start.37 = (f32[8,96]{1,0:T(8,128)S(1)}, f32[8,96]{1,0:T(8,128)}, u32[]{:S(2)}) copy-start(f32[8,96]{1,0:T(8,128)} %get-tuple-element.88) | copy-start | bytes 9220
  62.1 4.7 %copy-start.12 = (bf16[96,288]{1,0:T(8,128)(2,1)S(1)}, bf16[96,288]{1,0:T(8,128)(2,1)}, u32[]{:S(2)}) copy-start(bf16[96,288]{1,0:T(8,128)(2,1)} %get-tuple-element.113.refs_1_) | copy-start | bytes 165892
  63.0 19.4 %copy-start.9 = (bf16[8,96,288]{2,1,0:T(8,128)(2,1)S(1)}, bf16[8,96,288]{2,1,0:T(8,128)(2,1)}, u32[]{:S(2)}) copy-start(bf16[8,96,288]{2,1,0:T(8,128)(2,1)} %copy-done.8) | copy-start | bytes 1327108
  63.1 24.8 %copy-start.38 = (f32[128]{0:T(128)}, f32[128]{0:T(128)S(1)}, u32[]{:S(2)}) copy-start(f32[128]{0:T(128)S(1)} %broadcast_multiply_fusion.8) | copy-start | bytes 1540
  87.9 0.9 copy-start.6
  88.8 1.3 copy-start
  90.2 10.6 %copy-start.17 = (f32[128,768]{1,0:T(8,128)S(1)}, f32[128,768]{1,0:T(8,128)}, u32[]{:S(2)}) copy-start(f32[128,768]{1,0:T(8,128)} %get-tuple-element.93) | copy-start | bytes 1179652
  90.2 11.4 %copy-start.5 = (bf16[128,768]{1,0:T(8,128)(2,1)S(1)}, bf16[128,768]{1,0:T(8,128)(2,1)}, u32[]{:S(2)}) copy-start(bf16[128,768]{1,0:T(8,128)(2,1)} %refs_3_.1) | copy-start | bytes 589828
  101.6 2.9 %copy-start.1 = (bf16[768,896]{1,0:T(8,128)(2,1)S(1)}, bf16[768,896]{1,0:T(8,128)(2,1)}, u32[]{:S(2)}) copy-start(bf16[768,896]{1,0:T(8,128)(2,1)} %get-tuple-element.43) | copy-start | bytes 4128772
  104.5 15.2 %copy-start.16 = (f32[3,512,512]{1,2,0:T(8,128)S(1)}, f32[3,512,512]{1,2,0:T(8,128)}, u32[]{:S(2)}) copy-start(f32[3,512,512]{1,2,0:T(8,128)} %copy-done.15) | copy-start | bytes 9437188
  119.7 0.9 copy-start.24
  119.7 1.0 copy-start.26
  120.7 0.9 copy-start.28
  121.6 0.9 copy-start.30
  121.6 1.0 copy-start.33
  125.0 1.1 copy-start.22
  127.0 19.3 %copy-start.36 = (f32[768]{0:T(1024)S(1)}, f32[768]{0:T(1024)}, u32[]{:S(2)}) copy-start(f32[768]{0:T(1024)} %get-tuple-element.82) | copy-start | bytes 9220
  146.2 1.3 copy-start.39
  146.3 1.7 copy-start.14
  146.3 1.8 %copy-start.7 = (bf16[512,768]{1,0:T(8,128)(2,1)S(1)}, bf16[512,768]{1,0:T(8,128)(2,1)}, u32[]{:S(2)}) copy-start(bf16[512,768]{1,0:T(8,128)(2,1)} %copy-done.6) | copy-start | bytes 2359300
  146.5 0.9 copy-start.19
  148.0 19.6 %copy-start.18 = (f32[128,768]{1,0:T(8,128)S(1)}, f32[128,768]{1,0:T(8,128)}, u32[]{:S(2)}) copy-start(f32[128,768]{1,0:T(8,128)} %get-tuple-element.93) | copy-start | bytes 1179652
  148.1 20.2 %copy-start.20 = (f32[128,768]{1,0:T(8,128)S(1)}, f32[128,768]{1,0:T(8,128)}, u32[]{:S(2)}) copy-start(f32[128,768]{1,0:T(8,128)} %copy-done.19) | copy-start | bytes 1179652
  148.1 20.2 %copy-start.31 = (f32[128,768]{1,0:T(8,128)S(1)}, f32[128,768]{1,0:T(8,128)}, u32[]{:S(2)}) copy-start(f32[128,768]{1,0:T(8,128)} %get-tuple-element.91) | copy-start | bytes 1179652
  (8 other events, 6.5 us)
where the time goes:
time: 178 us; the launch traced here: 177 us
  Pallas kernels  134 us (75%)
  local copies, waits for them, and re-layouts  17.6 us (10%)
  other arithmetic  16.4 us (9%)
  matrix products  7.65 us (4%)
    pallas_call x8, Pallas kernels, exchange(): pl.pallas_call(functools.partial(exchange_kernel, plan, sizes), out_shape...  129 us
    unnamed x84, local copies, waits for them, and re-layouts  14 us
    pallas_call x1, Pallas kernels, feed_forward(): pl.pallas_call(functools.partial(feed_forward_kernel, hidden), out_shape=...  5.41 us
    dot_general x6, matrix products, dot_f32(): lax.dot_general(left, right, (((left_dim,), (right_dim,)), ((), ())), pre...  3.84 us

commit v1 on v0

--- a/solution.py
+++ b/solution.py
@@ -2,6 +2,7 @@
 
 import jax
 import jax.numpy as jnp
+import numpy as np
 from jax import lax
 from jax.experimental import pallas as pl
 from jax.experimental.pallas import tpu as pltpu
@@ -445,6 +446,560 @@
     )
 
 
+def lanes(shape, dim):
+    return lax.broadcasted_iota(jnp.int32, shape, dim)
+
+
+def spread_matrix(head_count, turned, sign):
+    shape = (head_count * HD, head_count * 2 * HD)
+    row, column = lanes(shape, 0), lanes(shape, 1)
+    head = lax.shift_right_logical(column, 7)
+    feature = lax.bitwise_and(column, HD - 1)
+    upper = lax.bitwise_and(column, 2 * HD - 1) >= HD
+    plain = row == head * HD + feature
+    if not turned:
+        return jnp.where(plain & jnp.logical_not(upper), 1.0, 0.0).astype(jnp.bfloat16)
+    other = row == head * HD + lax.bitwise_and(feature + HD // 2, HD - 1)
+    signed = jnp.where(feature < HD // 2, -sign, sign)
+    return jnp.where(
+        upper, jnp.where(other, signed, 0.0), jnp.where(plain, 1.0, 0.0)
+    ).astype(jnp.bfloat16)
+
+
+def paired_matrix():
+    shape = (2 * HD, 2 * HD)
+    row, column = lanes(shape, 0), lanes(shape, 1)
+    feature = lax.bitwise_and(column, HD - 1)
+    upper = column >= HD
+    other = row == lax.bitwise_and(feature + HD // 2, HD - 1)
+    signed = jnp.where(feature < HD // 2, 1.0, -1.0)
+    return jnp.where(
+        upper, jnp.where(other, signed, 0.0), jnp.where(row == column, 1.0, 0.0)
+    ).astype(jnp.bfloat16)
+
+
+def layer_kernel(sizes, dims, *refs):
+    bf16, f32 = jnp.bfloat16, jnp.float32
+    groups, members = sizes["dp"], sizes["tensor"]
+    own_rows, width, block, heads_wide, hidden, pad_hidden = dims
+    head_count = heads_wide // HD
+    spread = 2 * heads_wide
+    row_count = own_rows * members
+    outer, rings = groups // 2, members // 2
+    (
+        tok_in, cot_in, qkv_in, out_in, up_in, down_in, attn_in, mlp_in, table_in,
+        output_ref, input_grad_ref, gain_ref, qkv_grad_ref, out_grad_ref, mlp_grad_ref,
+        tok_buf, cot_buf, qkv_raw, out_raw, up_raw, down_raw, attn_raw, mlp_raw, table,
+        w_a, w_b, gain_buf, gain_rows, w_big, w_out_pad, up_w, gate_w, down_w,
+        rows_one, probs, q_buf, k_buf, v_buf, mix_t, mix, mix_pack,
+        part_one, recv_one, fwd_one, hidden_res, rows_two,
+        act_buf, up_grad, gate_grad, part_two, recv_two, fwd_two,
+        part_three, recv_three, fwd_three,
+        mlp_grads, mlp_half, mlp_sum, mlp_parts,
+        grad_hidden, grad_rows, out_grads, out_half, out_sum, out_parts,
+        proj_grad, qkv_grads, qkv_half, qkv_sum, qkv_parts,
+        part_four, recv_four, fwd_four, gain_send, gain_recv, gain_group,
+        load_sem, send_sem, recv_sem,
+    ) = refs
+    me_d, me_t = lax.axis_index("dp"), lax.axis_index("tensor")
+    zrow, col = me_d // 2, lax.rem(me_d, 2)
+    x_peer = zrow * 2 + 1 - col
+    yrow, core = me_t // 2, lax.rem(me_t, 2)
+    c_peer = yrow * 2 + 1 - core
+    counter = [0]
+    sent = []
+
+    def send(source, target, axis, peer):
+        index = counter[0]
+        counter[0] += 1
+        copy = pltpu.make_async_remote_copy(
+            src_ref=source,
+            dst_ref=target,
+            send_sem=send_sem.at[index],
+            recv_sem=recv_sem.at[index],
+            device_id={axis: peer},
+            device_id_type=pl.DeviceIdType.MESH,
+        )
+        copy.start()
+        sent.append(copy)
+        return copy
+
+    loads = [
+        pltpu.make_async_copy(source, target, load_sem.at[index])
+        for index, (source, target) in enumerate(
+            [
+                (qkv_in, qkv_raw), (out_in, out_raw), (attn_in, attn_raw), (mlp_in, mlp_raw),
+                (tok_in, tok_buf.at[me_t]), (cot_in, cot_buf.at[me_t]),
+                (up_in, up_raw), (down_in, down_raw), (table_in, table),
+            ]
+        )
+    ]
+    for load in loads:
+        load.start()
+    barrier = pltpu.get_barrier_semaphore()
+    for axis, me in (("dp", me_d), ("tensor", me_t)):
+        for shift in range(1, sizes[axis]):
+            pl.semaphore_signal(
+                barrier,
+                inc=1,
+                device_id={axis: lax.rem(me + shift, sizes[axis])},
+                device_id_type=pl.DeviceIdType.MESH,
+            )
+    eye_heads = jnp.where(
+        lanes((heads_wide, heads_wide), 0) == lanes((heads_wide, heads_wide), 1), 1.0, 0.0
+    ).astype(bf16)
+    eye_hidden = jnp.where(
+        lanes((hidden, hidden), 0) == lanes((hidden, hidden), 1), 1.0, 0.0
+    ).astype(bf16)
+    for load in loads[:4]:
+        load.wait()
+    gain_buf[me_d] = jnp.zeros(gain_buf.shape[1:], bf16)
+    gain_buf[me_d, 0:1, :block] = attn_raw[...]
+    gain_buf[me_d, 8:9, :block] = mlp_raw[...]
+    for which in range(3):
+        w_a[me_d, :, which * heads_wide : (which + 1) * heads_wide] = qkv_raw[which]
+    w_a[me_d, :, 3 * heads_wide :] = dot_f32(out_raw[...], eye_heads, 0, 0).astype(bf16)
+    for load in loads[4:]:
+        load.wait()
+    for which in range(2):
+        w_b[me_d, :, which * hidden : (which + 1) * hidden] = up_raw[which]
+    w_b[me_d, :, 2 * hidden : 3 * hidden] = dot_f32(down_raw[...], eye_hidden, 0, 0).astype(bf16)
+    if pad_hidden > 3 * hidden:
+        w_b[me_d, :, 3 * hidden :] = jnp.zeros((block, pad_hidden - 3 * hidden), bf16)
+    pl.semaphore_wait(barrier, groups + members - 2)
+
+    def dp_spread(buffer):
+        copies = []
+        for shift in range(1, outer):
+            peer = lax.rem(zrow + shift, outer) * 2 + col
+            origin = lax.rem(zrow + outer - shift, outer) * 2 + col
+            copies.append((send(buffer.at[me_d], buffer.at[me_d], "dp", peer), origin))
+        return copies
+
+    def dp_pair(buffer, origin):
+        mirrored = origin // 2 * 2 + 1 - col
+        return (send(buffer.at[origin], buffer.at[origin], "dp", x_peer), mirrored)
+
+    def tensor_spread(buffer):
+        copies = []
+        for shift in range(1, rings):
+            peer = lax.rem(yrow + shift, rings) * 2 + core
+            origin = lax.rem(yrow + rings - shift, rings) * 2 + core
+            copies.append((send(buffer.at[me_t], buffer.at[me_t], "tensor", peer), origin))
+        near = send(buffer.at[me_t], buffer.at[me_t], "tensor", c_peer)
+        return copies, near
+
+    def tensor_relay(buffer, copies):
+        onward = []
+        for copy, origin in copies:
+            copy.wait_recv()
+            onward.append(send(buffer.at[origin], buffer.at[origin], "tensor", c_peer))
+        return onward
+
+    gain_z = dp_spread(gain_buf)
+    gain_x = [dp_pair(gain_buf, me_d)]
+    a_z = dp_spread(w_a)
+    a_x = [dp_pair(w_a, me_d)]
+    tok_y, tok_near = tensor_spread(tok_buf)
+    cot_y, cot_near = tensor_spread(cot_buf)
+    b_z = dp_spread(w_b)
+
+    turn = spread_matrix(head_count, True, 1.0)
+    plain = spread_matrix(head_count, False, 1.0)
+
+    def expand(index):
+        for which, matrix in ((0, turn), (1, turn), (2, plain)):
+            piece = w_a[index, :, which * heads_wide : (which + 1) * heads_wide]
+            w_big[index, :, which * spread : (which + 1) * spread] = dot_f32(
+                piece, matrix, 1, 0
+            ).astype(bf16)
+        piece = w_a[index, :, 3 * heads_wide :]
+        w_out_pad[index] = dot_f32(piece, plain, 1, 0).astype(bf16)
+
+    for copy, origin in gain_z:
+        copy.wait_recv()
+        gain_x.append(dp_pair(gain_buf, origin))
+    expand(me_d)
+    tok_far = None
+    for number, (copy, origin) in enumerate(a_z):
+        copy.wait_recv()
+        a_x.append(dp_pair(w_a, origin))
+        expand(origin)
+        if number == 0:
+            tok_far = tensor_relay(tok_buf, tok_y)
+            cot_far = tensor_relay(cot_buf, cot_y)
+    b_x = [dp_pair(w_b, me_d)]
+    for copy, _ in gain_x:
+        copy.wait_recv()
+    for index in range(groups):
+        tile = gain_buf[index].astype(f32)
+        gain_rows[0:1, index * block : (index + 1) * block] = tile[0:1, :block]
+        gain_rows[8:9, index * block : (index + 1) * block] = tile[8:9, :block]
+    attn_gain, mlp_gain = gain_rows[0:1, :], gain_rows[8:9, :]
+    tok_near.wait_recv()
+    for copy in tok_far:
+        copy.wait_recv()
+    all_rows = tok_buf[...].reshape(row_count, width).astype(f32)
+    rows_one[...] = (normalize(all_rows)[0] * attn_gain).astype(bf16)
+    for copy, mirrored in a_x:
+        copy.wait_recv()
+        expand(mirrored)
+
+    paired = paired_matrix()
+    rotary = table[...]
+    for which in range(3):
+        weight = w_big[:, :, which * spread : (which + 1) * spread].reshape(width, spread)
+        projected = dot_f32(rows_one[...], weight, 1, 0)
+        for head in range(head_count):
+            piece = projected[:, head * 128 : (head + 1) * 128]
+            if which == 2:
+                v_buf[head] = piece.astype(bf16)
+                continue
+            turned = piece * rotary
+            turned = (turned + pltpu.roll(turned, 64, 1)).astype(bf16)
+            (q_buf, k_buf)[which][head] = turned
+    for head in range(head_count):
+        scores = dot_f32(k_buf[head], q_buf[head], 1, 1) * (0.5 * HD ** (-0.5))
+        peak = jnp.max(scores, axis=0, keepdims=True)
+        powers = jnp.exp(scores - peak)
+        share = powers * (1.0 / jnp.sum(powers, axis=0, keepdims=True))
+        probs[head] = share
+        mixed_t = dot_f32(v_buf[head], share.astype(bf16), 0, 0).astype(bf16)
+        mix_t[head] = mixed_t
+        mixed = jnp.transpose(mixed_t.astype(f32)).astype(bf16)
+        mix[:, :, head * 128 : (head + 1) * 128] = mixed.reshape(members, own_rows, 128)
+        mix_pack[:, head * HD : (head + 1) * HD] = mixed[:, :HD]
+
+    def reduce_start(part, recv):
+        first = []
+        for shift in range(1, rings):
+            far = lax.rem(yrow + shift, rings)
+            first.append(send(part.at[far * 2 + 1 - core], recv.at[shift], "tensor", c_peer))
+        return first, send(part.at[c_peer], recv.at[0], "tensor", c_peer)
+
+    def reduce_middle(part, recv, fwd, first):
+        second = []
+        for shift in range(1, rings):
+            far = lax.rem(yrow + shift, rings)
+            first[shift - 1].wait_recv()
+            fwd[shift] = (part[far * 2 + core].astype(f32) + recv[shift].astype(f32)).astype(bf16)
+            second.append(
+                send(fwd.at[shift], recv.at[rings + shift], "tensor", far * 2 + core)
+            )
+        return second
+
+    def reduce_finish(part, recv, near, second):
+        near.wait_recv()
+        total = part[me_t].astype(f32) + recv[0].astype(f32)
+        for shift in range(1, rings):
+            second[shift - 1].wait_recv()
+            total = total + recv[rings + shift].astype(f32)
+        return total
+
+    out_weight = w_out_pad[...].reshape(width, spread)
+    part_one[...] = (
+        dot_f32(mix[...].reshape(row_count, spread), out_weight, 1, 1)
+        .astype(bf16)
+        .reshape(members, own_rows, width)
+    )
+    first_one, near_one = reduce_start(part_one, recv_one)
+    second_one = reduce_middle(part_one, recv_one, fwd_one, first_one)
+    for copy, origin in b_z:
+        copy.wait_recv()
+        b_x.append(dp_pair(w_b, origin))
+    for head in range(head_count):
+        q_buf[head] = dot_f32(q_buf[head], paired, 1, 0).astype(bf16)
+        k_buf[head] = dot_f32(k_buf[head], paired, 1, 0).astype(bf16)
+    residual = tok_buf[me_t].astype(f32)
+    hidden_res[...] = residual + reduce_finish(part_one, recv_one, near_one, second_one)
+    normed_two, inv_two = normalize(hidden_res[...])
+    rows_two[me_t] = (normed_two * mlp_gain).astype(bf16)
+    rows_y, rows_near = tensor_spread(rows_two)
+    cot_near.wait_recv()
+    for copy in cot_far:
+        copy.wait_recv()
+    for copy, _ in b_x:
+        copy.wait_recv()
+    up_w[...] = w_b[:, :, :hidden].reshape(width, hidden)
+    gate_w[...] = w_b[:, :, hidden : 2 * hidden].reshape(width, hidden)
+    down_w[...] = w_b[:, :, 2 * hidden : 3 * hidden].reshape(width, hidden)
+
+    def feed(ring):
+        base = 2 * ring
+        count = 2 * own_rows
+        rows = rows_two[pl.ds(base, 2)].reshape(count, width)
+        cot = cot_buf[pl.ds(base, 2)].reshape(count, width)
+        inputs = dot_f32(rows, up_w[...], 1, 0)
+        gate_part = dot_f32(rows, gate_w[...], 1, 0)
+        grad_act = dot_f32(cot, down_w[...], 1, 0)
+        activated, slope = gelu_pair(inputs)
+        act_buf[ring] = (activated * gate_part).astype(bf16)
+        grad_up = (grad_act * gate_part * slope).astype(bf16)
+        grad_gate = (grad_act * activated).astype(bf16)
+        up_grad[ring] = grad_up
+        gate_grad[ring] = grad_gate
+        part_two[pl.ds(base, 2)] = (
+            (dot_f32(grad_up, up_w[...], 1, 1) + dot_f32(grad_gate, gate_w[...], 1, 1))
+            .astype(bf16)
+            .reshape(2, own_rows, width)
+        )
+
+    rows_near.wait_recv()
+    feed(yrow)
+    rows_far = tensor_relay(rows_two, rows_y)
+    for copy in rows_far:
+        copy.wait_recv()
+    for shift in range(1, rings):
+        feed(lax.rem(yrow + shift, rings))
+    first_two, near_two = reduce_start(part_two, recv_two)
+    second_two = reduce_middle(part_two, recv_two, fwd_two, first_two)
+
+    def pair_start(grads, half):
+        copies = []
+        for shift in range(1, outer + 1):
+            row = lax.rem(zrow + shift, outer)
+            copies.append((send(grads.at[row * 2 + 1 - col], half.at[row], "dp", x_peer), row))
+        return copies
+
+    def pair_finish(grads, half, sums, parts, copies):
+        across = []
+        for number, (copy, row) in enumerate(copies):
+            copy.wait_recv()
+            value = (grads[row * 2 + col].astype(f32) + half[row].astype(f32)).astype(bf16)
+            if number == outer - 1:
+                parts[row] = value
+                continue
+            sums[row] = value
+            across.append(send(sums.at[row], parts.at[zrow], "dp", row * 2 + col))
+        return across
+
+    full_rows = rows_two[...].reshape(row_count, width)
+    full_cot = cot_buf[...].reshape(row_count, width)
+    for which, grad in ((0, up_grad), (1, gate_grad)):
+        mlp_grads[:, :, which * hidden : (which + 1) * hidden] = (
+            dot_f32(full_rows, grad[...].reshape(row_count, hidden), 0, 0)
+            .astype(bf16)
+            .reshape(groups, block, hidden)
+        )
+    full_act = act_buf[...].reshape(row_count, hidden)
+    mlp_grads[:, :, 2 * hidden : 3 * hidden] = (
+        dot_f32(full_cot, full_act, 0, 0).astype(bf16).reshape(groups, block, hidden)
+    )
+    if pad_hidden > 3 * hidden:
+        mlp_grads[:, :, 3 * hidden :] = jnp.zeros(
+            (groups, block, pad_hidden - 3 * hidden), bf16
+        )
+    mlp_pairs = pair_start(mlp_grads, mlp_half)
+    part_three[...] = (
+        dot_f32(full_act, down_w[...], 1, 1).astype(bf16).reshape(members, own_rows, width)
+    )
+    normed_two, inv_two = normalize(hidden_res[...])
+    back_two = reduce_finish(part_two, recv_two, near_two, second_two)
+    grad_res, mlp_gain_part = normalize_back(back_two, normed_two, inv_two, mlp_gain)
+    grad_hidden[...] = cot_buf[me_t].astype(f32) + grad_res
+    grad_rows[me_t] = grad_hidden[...].astype(bf16)
+    grad_y, grad_near = tensor_spread(grad_rows)
+    first_three, near_three = reduce_start(part_three, recv_three)
+    grad_far = tensor_relay(grad_rows, grad_y)
+    second_three = reduce_middle(part_three, recv_three, fwd_three, first_three)
+    grad_near.wait_recv()
+    for copy in grad_far:
+        copy.wait_recv()
+    full_grad = grad_rows[...].reshape(row_count, width)
+    grad_mix = dot_f32(full_grad, out_weight, 1, 0).astype(bf16)
+    out_grads[...] = (
+        dot_f32(full_grad, mix_pack[...], 0, 0).astype(bf16).reshape(groups, block, heads_wide)
+    )
+    mlp_across = pair_finish(mlp_grads, mlp_half, mlp_sum, mlp_parts, mlp_pairs)
+    out_pairs = pair_start(out_grads, out_half)
+    scale = HD ** (-0.5)
+    for head in range(head_count):
+        grad_head = grad_mix[:, head * 128 : (head + 1) * 128]
+        grad_head_t = jnp.transpose(grad_head.astype(f32))
+        delta = jnp.sum(grad_head_t * mix_t[head].astype(f32), axis=0, keepdims=True)
+        grad_probs = dot_f32(v_buf[head], grad_head, 1, 1)
+        share = probs[head]
+        grad_scores = (share * (grad_probs - delta)).astype(bf16)
+        grad_v = dot_f32(share.astype(bf16), grad_head, 1, 0)
+        grad_k = dot_f32(grad_scores, q_buf[head], 1, 0) * (rotary * scale)
+        grad_k = grad_k + pltpu.roll(grad_k, 64, 1)
+        grad_q = jnp.transpose(dot_f32(k_buf[head], grad_scores, 0, 0)) * (rotary * scale)
+        grad_q = grad_q + pltpu.roll(grad_q, 64, 1)
+        for which, value in enumerate((grad_q, grad_k, grad_v)):
+            start = which * heads_wide + head * HD
+            proj_grad[:, start : start + HD] = value[:, :HD].astype(bf16)
+    out_across = pair_finish(out_grads, out_half, out_sum, out_parts, out_pairs)
+    qkv_grads[...] = (
+        dot_f32(rows_one[...], proj_grad[...], 0, 0)
+        .astype(bf16)
+        .reshape(groups, block, 3 * heads_wide)
+    )
+    qkv_pairs = pair_start(qkv_grads, qkv_half)
+    qkv_weight = w_a[:, :, : 3 * heads_wide].reshape(width, 3 * heads_wide)
+    part_four[...] = (
+        dot_f32(proj_grad[...], qkv_weight, 1, 1)
+        .astype(bf16)
+        .reshape(members, own_rows, width)
+    )
+    first_four, near_four = reduce_start(part_four, recv_four)
+    second_four = reduce_middle(part_four, recv_four, fwd_four, first_four)
+
+    def total(parts, across):
+        for copy in across:
+            copy.wait_recv()
+        return jnp.sum(parts[...].astype(f32), axis=0)
+
+    mlp_out = reduce_finish(part_three, recv_three, near_three, second_three)
+    output_ref[...] = (hidden_res[...] + mlp_out).astype(bf16)
+    qkv_across = pair_finish(qkv_grads, qkv_half, qkv_sum, qkv_parts, qkv_pairs)
+    residual = tok_buf[me_t].astype(f32)
+    normed_one, inv_one = normalize(residual)
+    back_one = reduce_finish(part_four, recv_four, near_four, second_four)
+    grad_res, attn_gain_part = normalize_back(back_one, normed_one, inv_one, attn_gain)
+    input_grad_ref[...] = grad_hidden[...] + grad_res
+    gain_send[...] = jnp.zeros(gain_send.shape, f32)
+    attn_row = attn_gain_part.reshape(1, width)
+    mlp_row = mlp_gain_part.reshape(1, width)
+    for index in range(groups):
+        gain_send[index, 0:1, :block] = attn_row[:, index * block : (index + 1) * block]
+        gain_send[index, 1:2, :block] = mlp_row[:, index * block : (index + 1) * block]
+    gain_recv[me_d] = gain_send[me_d]
+    gain_copies = []
+    for shift in range(1, groups):
+        peer = lax.rem(me_d + shift, groups)
+        gain_copies.append(send(gain_send.at[peer], gain_recv.at[me_d], "dp", peer))
+    mlp_grad_ref[...] = total(mlp_parts, mlp_across)
+    out_grad_ref[...] = total(out_parts, out_across)
+    gain_group[me_t] = total(gain_recv, gain_copies)
+    gain_copies = []
+    for shift in range(1, members):
+        peer = lax.rem(me_t + shift, members)
+        gain_copies.append(send(gain_group.at[me_t], gain_group.at[me_t], "tensor", peer))
+    qkv_grad_ref[...] = total(qkv_parts, qkv_across)
+    gain_ref[...] = total(gain_group, gain_copies)
+    for copy in sent:
+        copy.wait_send()
+
+
+def rotary_table(row_count):
+    position = (np.arange(row_count) % L).astype(np.float32)
+    halves = np.arange(HD // 2).astype(np.float32)
+    inverse = np.float32(ROPE_THETA) ** (np.float32(-2.0) * halves / np.float32(HD))
+    angles = position[:, None] * inverse[None, :]
+    return np.concatenate([np.cos(angles)] * 2 + [np.sin(angles)] * 2, axis=1).astype(np.float32)
+
+
+def whole_layer(sizes, tokens, attn_gain, w_qkv, w_out, mlp_gain, w_in, w_down, cotangent):
+    bf16, f32 = jnp.bfloat16, jnp.float32
+    groups, members = sizes["dp"], sizes["tensor"]
+    own_rows, width = tokens.shape
+    block, heads_wide, hidden = w_qkv.shape[1], w_qkv.shape[2], w_in.shape[2]
+    pad_hidden = -(-3 * hidden // 128) * 128
+    row_count = own_rows * members
+    head_count, spread = heads_wide // HD, 2 * heads_wide
+    outer, rings = groups // 2, members // 2
+    vmem = pltpu.VMEM
+    parts = vmem((members, own_rows, width), bf16)
+    arrived = vmem((2 * rings, own_rows, width), bf16)
+    passed = vmem((rings, own_rows, width), bf16)
+    heads = vmem((head_count, row_count, 128), bf16)
+    ringed = vmem((rings, 2 * own_rows, hidden), bf16)
+
+    def exchanged(wide):
+        quarter = vmem((outer, block, wide), bf16)
+        return [vmem((groups, block, wide), bf16), quarter, quarter, quarter]
+
+    scratch = [
+        parts, parts,
+        vmem(w_qkv.shape, bf16), vmem(w_out.shape, bf16),
+        vmem(w_in.shape, bf16), vmem(w_down.shape, bf16),
+        vmem((1, block), bf16), vmem((1, block), bf16), vmem((row_count, 2 * HD), f32),
+        vmem((groups, block, 4 * heads_wide), bf16),
+        vmem((groups, block, pad_hidden), bf16),
+        vmem((groups, 16, 128), bf16),
+        vmem((16, width), f32),
+        vmem((groups, block, 3 * spread), bf16),
+        vmem((groups, block, spread), bf16),
+        vmem((width, hidden), bf16), vmem((width, hidden), bf16), vmem((width, hidden), bf16),
+        vmem((row_count, width), bf16),
+        vmem((head_count, row_count, row_count), f32),
+        heads, heads, heads,
+        vmem((head_count, 128, row_count), bf16),
+        vmem((members, own_rows, spread), bf16),
+        vmem((row_count, heads_wide), bf16),
+        parts, arrived, passed,
+        vmem((own_rows, width), f32),
+        parts,
+        ringed, ringed, ringed,
+        parts, arrived, passed,
+        parts, arrived, passed,
+        *exchanged(pad_hidden),
+        vmem((own_rows, width), f32),
+        parts,
+        *exchanged(heads_wide),
+        vmem((row_count, 3 * heads_wide), bf16),
+        *exchanged(3 * heads_wide),
+        parts, arrived, passed,
+        vmem((groups, 8, 128), f32), vmem((groups, 8, 128), f32), vmem((members, 8, 128), f32),
+    ]
+    gathers = 3 * (2 * outer - 1) + 4 * (2 * rings - 1)
+    reduces = 4 * (2 * rings - 1) + 3 * (2 * outer - 1)
+    slots = gathers + reduces + groups + members - 2
+    dims = (own_rows, width, block, heads_wide, hidden, pad_hidden)
+    output, input_grad, gains, qkv_sum, out_sum, mlp_sums = pl.pallas_call(
+        functools.partial(layer_kernel, sizes, dims),
+        out_shape=[
+            jax.ShapeDtypeStruct((own_rows, width), bf16),
+            jax.ShapeDtypeStruct((own_rows, width), f32),
+            jax.ShapeDtypeStruct((8, 128), f32),
+            jax.ShapeDtypeStruct((block, 3 * heads_wide), f32),
+            jax.ShapeDtypeStruct((block, heads_wide), f32),
+            jax.ShapeDtypeStruct((block, pad_hidden), f32),
+        ],
+        in_specs=[pl.BlockSpec(memory_space=pl.ANY)] * 9,
+        out_specs=[pl.BlockSpec(memory_space=pltpu.VMEM)] * 6,
+        scratch_shapes=scratch
+        + [
+            pltpu.SemaphoreType.DMA((9,)),
+            pltpu.SemaphoreType.DMA((slots,)),
+            pltpu.SemaphoreType.DMA((slots,)),
+        ],
+        compiler_params=pltpu.CompilerParams(
+            collective_id=0, has_side_effects=True, vmem_limit_bytes=60 << 20
+        ),
+    )(
+        tokens, cotangent, w_qkv, w_out, w_in, w_down,
+        attn_gain.reshape(1, block), mlp_gain.reshape(1, block),
+        jnp.asarray(rotary_table(row_count)),
+    )
+    grad_w_qkv = jnp.stack(
+        [qkv_sum[:, i * heads_wide : (i + 1) * heads_wide] for i in range(3)]
+    )
+    grad_w_in = jnp.stack([mlp_sums[:, :hidden], mlp_sums[:, hidden : 2 * hidden]])
+    return (
+        output,
+        input_grad,
+        gains[0, :block],
+        grad_w_qkv,
+        out_sum.T,
+        gains[1, :block],
+        grad_w_in,
+        mlp_sums[:, 2 * hidden : 3 * hidden].T,
+    )
+
+
+def fits_whole(sizes, tokens, w_qkv):
+    row_count = tokens.shape[0] * sizes["tensor"]
+    even = sizes["dp"] % 2 == 0 and sizes["tensor"] % 2 == 0
+    tiled = w_qkv.shape[1] % 16 == 0 and tokens.shape[0] % 16 == 0
+    return even and tiled and row_count == L and w_qkv.shape[1] <= 128
+
+
+def layer(sizes, tokens, attn_gain, w_qkv, *rest):
+    run = whole_layer if fits_whole(sizes, tokens, w_qkv) else body
+    return run(sizes, tokens, attn_gain, w_qkv, *rest)
+
+
 def solution(mesh):
     in_specs = (
         P(("dp", "tensor"), None),
@@ -467,4 +1022,4 @@
         P("tensor", "dp"),
     )
     sizes = {axis: mesh.shape[axis] for axis in ("dp", "tensor")}
-    return jax.shard_map(functools.partial(body, sizes), mesh=mesh, in_specs=in_specs, out_specs=out_specs, check_vma=False)
+    return jax.shard_map(functools.partial(layer, sizes), mesh=mesh, in_specs=in_specs, out_specs=out_specs, check_vma=False)

time: 178 us -> 116 us (0.65)
  the two profiles are of different devices: /device:TPU:0 before, /device:TPU:27 now
where the time goes in v1:
time: 116 us; the launch traced here: 115 us
  Pallas kernels  106 us (91%)
  local copies, waits for them, and re-layouts  6.99 us (6%)
  other arithmetic  1.47 us (1%)
    pallas_call x1, Pallas kernels, whole_layer(): pl.pallas_call(functools.partial(layer_kernel, sizes, dims), out_shape=[j...  106 us
    unnamed x10, local copies, waits for them, and re-layouts  4.48 us

profile of v1, /device:TPU:27, one launch (start us, length us, event | category | flops | bytes accessed | tf_op | source)
XLA Modules:
  0.0 115.4 jit_solution(15686313681148217582)
XLA Ops:
  0.6 106.3 %shard_map.152 = (bf16[128,768]{1,0:T(8,128)(2,1)}, f32[128,768]{1,0:T(8,128)}, f32[8,128]{1,0:T(8,128)}, f32[96,576]{1,0:T(8,128)}, f32[96,192]{1,0:T(8,128)}, /*index=5*/f32[96,896]{1,0:T(8,128)}) custom-call(bf16[128,768]{1,0:T(8,128)(2,1)} %refs_0_.1, bf16[128,768]{1,0:T(8,128)(2,1)} %refs_1_.1, bf16[3,96,192]{2,1,0:T(8,128)(2,1)} %refs_2_.1, ...), custom_call_target="tpu_custom_call" | custom-call | tf_op jit(solution)/shard_map/pallas_call | solution.py:949
  106.9 1.3 %slice_bitcast_fusion.6 = (f32[96]{0:T(128)}, f32[96]{0:T(128)}) fusion(f32[8,128]{1,0:T(8,128)} %get-tuple-element.16), kind=kLoop, calls=%fused_computation.8 | loop fusion | bytes 1536 | tf_op jit(solution)/shard_map/squeeze | solution.py:985
  108.2 1.6 %copy.17 = f32[192,96]{1,0:T(8,128)} copy(f32[192,96]{0,1:T(8,128)} %bitcast.19) | data formatting | bytes 147456
  109.9 1.1 slice_bitcast_fusion.5
  111.0 0.0 copy-start
  111.0 0.7 pad_maximum_fusion
  111.7 0.3 copy-done
  112.0 0.1 slice_bitcast_fusion
  112.2 0.8 copy.18
  113.0 0.0 copy-start.2
  113.0 0.0 copy-start.1
  113.0 0.7 pad_maximum_fusion.1
  113.7 0.3 copy-done.2
  114.0 0.7 copy.21
  114.7 0.0 copy-done.1
  114.7 0.7 copy.22
Async XLA Ops:
  111.0 1.1 copy-start
  113.0 1.0 copy-start.2
  113.0 1.7 %copy-start.1 = (f32[128,768]{1,0:T(8,128)S(1)}, f32[128,768]{1,0:T(8,128)}, u32[]{:S(2)}) copy-start(f32[128,768]{1,0:T(8,128)} %get-tuple-element.45) | copy-start | bytes 1179652

commit v2 on v1

--- a/solution.py
+++ b/solution.py
@@ -509,10 +509,10 @@
     counter = [0]
     sent = []
 
-    def send(source, target, axis, peer):
+    def make(source, target, axis, peer):
         index = counter[0]
         counter[0] += 1
-        copy = pltpu.make_async_remote_copy(
+        return pltpu.make_async_remote_copy(
             src_ref=source,
             dst_ref=target,
             send_sem=send_sem.at[index],
@@ -520,9 +520,84 @@
             device_id={axis: peer},
             device_id_type=pl.DeviceIdType.MESH,
         )
+
+    def send(source, target, axis, peer):
+        copy = make(source, target, axis, peer)
         copy.start()
-        sent.append(copy)
+        sent.append((copy, None))
         return copy
+
+    def begin(copy, condition):
+        pl.when(condition)(copy.start)
+        sent.append((copy, condition))
+
+    cuts = 2 if block % 32 == 0 else 1
+    height = block // cuts
+
+    class Chain:
+        def __init__(self, buffer):
+            self.buffer = buffer
+            self.moves = {}
+            last = outer - 1
+            for step in range(1, outer):
+                for side in (0, 1):
+                    ahead = 1 if side == 0 else outer - 1
+                    target = lax.rem(zrow + ahead, outer) * 2 + col
+                    back = step - 1 if side else outer - step + 1
+                    carried = lax.rem(zrow + back, outer) * 2 + col
+                    origin = lax.rem(zrow + (step if side else outer - step), outer) * 2
+                    lands = zrow + step <= last if side else zrow >= step
+                    starts = (
+                        (zrow >= 1) & (zrow + step - 1 <= last)
+                        if side
+                        else (zrow < last) & (zrow >= step - 1)
+                    )
+                    for cut in range(cuts):
+                        self.moves[step, side, cut] = (
+                            make(self.piece(carried, cut), self.piece(carried, cut), "dp", target),
+                            make(
+                                self.piece(origin + col, cut),
+                                self.piece(origin + col, cut),
+                                "dp",
+                                x_peer,
+                            ),
+                            starts,
+                            lands,
+                            origin,
+                        )
+
+        def piece(self, index, cut):
+            return self.buffer.at[index, cut * height : (cut + 1) * height]
+
+        def start(self):
+            self.own = []
+            for cut in range(cuts):
+                for side in (0, 1):
+                    move, _, starts, _, _ = self.moves[1, side, cut]
+                    begin(move, starts)
+                piece = self.piece(me_d, cut)
+                self.own.append(send(piece, piece, "dp", x_peer))
+
+        def step(self, number):
+            for cut in range(cuts):
+                for side in (0, 1):
+                    move, across, _, lands, _ = self.moves[number, side, cut]
+                    pl.when(lands)(move.wait_recv)
+                    if number + 1 < outer:
+                        onward, _, starts, _, _ = self.moves[number + 1, side, cut]
+                        begin(onward, starts)
+                    begin(across, lands)
+
+        def paired(self, number, then=None):
+            for side in (0, 1):
+                lands, origin = self.moves[number, side, 0][3:]
+
+                @pl.when(lands)
+                def _():
+                    for cut in range(cuts):
+                        self.moves[number, side, cut][1].wait_recv()
+                    if then is not None:
+                        then(origin + 1 - col)
 
     loads = [
         pltpu.make_async_copy(source, target, load_sem.at[index])
@@ -548,9 +623,6 @@
     eye_heads = jnp.where(
         lanes((heads_wide, heads_wide), 0) == lanes((heads_wide, heads_wide), 1), 1.0, 0.0
     ).astype(bf16)
-    eye_hidden = jnp.where(
-        lanes((hidden, hidden), 0) == lanes((hidden, hidden), 1), 1.0, 0.0
-    ).astype(bf16)
     for load in loads[:4]:
         load.wait()
     gain_buf[me_d] = jnp.zeros(gain_buf.shape[1:], bf16)
@@ -559,13 +631,6 @@
     for which in range(3):
         w_a[me_d, :, which * heads_wide : (which + 1) * heads_wide] = qkv_raw[which]
     w_a[me_d, :, 3 * heads_wide :] = dot_f32(out_raw[...], eye_heads, 0, 0).astype(bf16)
-    for load in loads[4:]:
-        load.wait()
-    for which in range(2):
-        w_b[me_d, :, which * hidden : (which + 1) * hidden] = up_raw[which]
-    w_b[me_d, :, 2 * hidden : 3 * hidden] = dot_f32(down_raw[...], eye_hidden, 0, 0).astype(bf16)
-    if pad_hidden > 3 * hidden:
-        w_b[me_d, :, 3 * hidden :] = jnp.zeros((block, pad_hidden - 3 * hidden), bf16)
     pl.semaphore_wait(barrier, groups + members - 2)
 
     def dp_spread(buffer):
@@ -598,11 +663,23 @@
 
     gain_z = dp_spread(gain_buf)
     gain_x = [dp_pair(gain_buf, me_d)]
-    a_z = dp_spread(w_a)
-    a_x = [dp_pair(w_a, me_d)]
+    chain_a = Chain(w_a)
+    chain_a.start()
+    for load in loads[4:6]:
+        load.wait()
     tok_y, tok_near = tensor_spread(tok_buf)
     cot_y, cot_near = tensor_spread(cot_buf)
-    b_z = dp_spread(w_b)
+    for load in loads[6:]:
+        load.wait()
+    eye_hidden = jnp.where(
+        lanes((hidden, hidden), 0) == lanes((hidden, hidden), 1), 1.0, 0.0
+    ).astype(bf16)
+    for which in range(2):
+        w_b[me_d, :, which * hidden : (which + 1) * hidden] = up_raw[which]
+    w_b[me_d, :, 2 * hidden : 3 * hidden] = dot_f32(down_raw[...], eye_hidden, 0, 0).astype(bf16)
+    if pad_hidden > 3 * hidden:
+        w_b[me_d, :, 3 * hidden :] = jnp.zeros((block, pad_hidden - 3 * hidden), bf16)
+    chain_b = Chain(w_b)
 
     turn = spread_matrix(head_count, True, 1.0)
     plain = spread_matrix(head_count, False, 1.0)
@@ -616,19 +693,14 @@
         piece = w_a[index, :, 3 * heads_wide :]
         w_out_pad[index] = dot_f32(piece, plain, 1, 0).astype(bf16)
 
+    expand(me_d)
+    chain_a.step(1)
     for copy, origin in gain_z:
         copy.wait_recv()
         gain_x.append(dp_pair(gain_buf, origin))
-    expand(me_d)
-    tok_far = None
-    for number, (copy, origin) in enumerate(a_z):
-        copy.wait_recv()
-        a_x.append(dp_pair(w_a, origin))
-        expand(origin)
-        if number == 0:
-            tok_far = tensor_relay(tok_buf, tok_y)
-            cot_far = tensor_relay(cot_buf, cot_y)
-    b_x = [dp_pair(w_b, me_d)]
+    tok_far = tensor_relay(tok_buf, tok_y)
+    for number in range(2, outer - 1):
+        chain_a.step(number)
     for copy, _ in gain_x:
         copy.wait_recv()
     for index in range(groups):
@@ -641,9 +713,17 @@
         copy.wait_recv()
     all_rows = tok_buf[...].reshape(row_count, width).astype(f32)
     rows_one[...] = (normalize(all_rows)[0] * attn_gain).astype(bf16)
-    for copy, mirrored in a_x:
+    if outer > 2:
+        chain_a.step(outer - 1)
+    chain_b.start()
+    cot_far = tensor_relay(cot_buf, cot_y)
+    for shift in range(1, outer):
+        expand(lax.rem(zrow + shift, outer) * 2 + col)
+    for copy in chain_a.own:
         copy.wait_recv()
-        expand(mirrored)
+    expand(x_peer)
+    for number in range(1, outer):
+        chain_a.paired(number, expand)
 
     paired = paired_matrix()
     rotary = table[...]
@@ -658,6 +738,7 @@
             turned = piece * rotary
             turned = (turned + pltpu.roll(turned, 64, 1)).astype(bf16)
             (q_buf, k_buf)[which][head] = turned
+    chain_b.step(1)
     for head in range(head_count):
         scores = dot_f32(k_buf[head], q_buf[head], 1, 1) * (0.5 * HD ** (-0.5))
         peak = jnp.max(scores, axis=0, keepdims=True)
@@ -704,9 +785,8 @@
     )
     first_one, near_one = reduce_start(part_one, recv_one)
     second_one = reduce_middle(part_one, recv_one, fwd_one, first_one)
-    for copy, origin in b_z:
-        copy.wait_recv()
-        b_x.append(dp_pair(w_b, origin))
+    for number in range(2, outer - 1):
+        chain_b.step(number)
     for head in range(head_count):
         q_buf[head] = dot_f32(q_buf[head], paired, 1, 0).astype(bf16)
         k_buf[head] = dot_f32(k_buf[head], paired, 1, 0).astype(bf16)
@@ -715,11 +795,15 @@
     normed_two, inv_two = normalize(hidden_res[...])
     rows_two[me_t] = (normed_two * mlp_gain).astype(bf16)
     rows_y, rows_near = tensor_spread(rows_two)
+    if outer > 2:
+        chain_b.step(outer - 1)
     cot_near.wait_recv()
     for copy in cot_far:
         copy.wait_recv()
-    for copy, _ in b_x:
+    for copy in chain_b.own:
         copy.wait_recv()
+    for number in range(1, outer):
+        chain_b.paired(number)
     up_w[...] = w_b[:, :, :hidden].reshape(width, hidden)
     gate_w[...] = w_b[:, :, hidden : 2 * hidden].reshape(width, hidden)
     down_w[...] = w_b[:, :, 2 * hidden : 3 * hidden].reshape(width, hidden)
@@ -745,8 +829,8 @@
         )
 
     rows_near.wait_recv()
+    rows_far = tensor_relay(rows_two, rows_y)
     feed(yrow)
-    rows_far = tensor_relay(rows_two, rows_y)
     for copy in rows_far:
         copy.wait_recv()
     for shift in range(1, rings):
@@ -761,17 +845,15 @@
             copies.append((send(grads.at[row * 2 + 1 - col], half.at[row], "dp", x_peer), row))
         return copies
 
-    def pair_finish(grads, half, sums, parts, copies):
-        across = []
-        for number, (copy, row) in enumerate(copies):
-            copy.wait_recv()
-            value = (grads[row * 2 + col].astype(f32) + half[row].astype(f32)).astype(bf16)
-            if number == outer - 1:
-                parts[row] = value
-                continue
-            sums[row] = value
-            across.append(send(sums.at[row], parts.at[zrow], "dp", row * 2 + col))
-        return across
+    def pair_step(grads, half, sums, parts, copies, number):
+        copy, row = copies[number]
+        copy.wait_recv()
+        value = (grads[row * 2 + col].astype(f32) + half[row].astype(f32)).astype(bf16)
+        if number == outer - 1:
+            parts[row] = value
+            return []
+        sums[row] = value
+        return [send(sums.at[row], parts.at[zrow], "dp", row * 2 + col)]
 
     full_rows = rows_two[...].reshape(row_count, width)
     full_cot = cot_buf[...].reshape(row_count, width)
@@ -800,6 +882,8 @@
     grad_rows[me_t] = grad_hidden[...].astype(bf16)
     grad_y, grad_near = tensor_spread(grad_rows)
     first_three, near_three = reduce_start(part_three, recv_three)
+    mlp_state = (mlp_grads, mlp_half, mlp_sum, mlp_parts, mlp_pairs)
+    mlp_across = pair_step(*mlp_state, 0)
     grad_far = tensor_relay(grad_rows, grad_y)
     second_three = reduce_middle(part_three, recv_three, fwd_three, first_three)
     grad_near.wait_recv()
@@ -810,8 +894,9 @@
     out_grads[...] = (
         dot_f32(full_grad, mix_pack[...], 0, 0).astype(bf16).reshape(groups, block, heads_wide)
     )
-    mlp_across = pair_finish(mlp_grads, mlp_half, mlp_sum, mlp_parts, mlp_pairs)
     out_pairs = pair_start(out_grads, out_half)
+    for number in range(1, outer - 2):
+        mlp_across += pair_step(*mlp_state, number)
     scale = HD ** (-0.5)
     for head in range(head_count):
         grad_head = grad_mix[:, head * 128 : (head + 1) * 128]
@@ -828,7 +913,6 @@
         for which, value in enumerate((grad_q, grad_k, grad_v)):
             start = which * heads_wide + head * HD
             proj_grad[:, start : start + HD] = value[:, :HD].astype(bf16)
-    out_across = pair_finish(out_grads, out_half, out_sum, out_parts, out_pairs)
     qkv_grads[...] = (
         dot_f32(rows_one[...], proj_grad[...], 0, 0)
         .astype(bf16)
@@ -849,9 +933,16 @@
             copy.wait_recv()
         return jnp.sum(parts[...].astype(f32), axis=0)
 
+    for number in range(max(outer - 2, 1), outer):
+        mlp_across += pair_step(*mlp_state, number)
     mlp_out = reduce_finish(part_three, recv_three, near_three, second_three)
     output_ref[...] = (hidden_res[...] + mlp_out).astype(bf16)
-    qkv_across = pair_finish(qkv_grads, qkv_half, qkv_sum, qkv_parts, qkv_pairs)
+    out_state = (out_grads, out_half, out_sum, out_parts, out_pairs)
+    out_across = []
+    for number in range(outer):
+        out_across += pair_step(*out_state, number)
+    qkv_state = (qkv_grads, qkv_half, qkv_sum, qkv_parts, qkv_pairs)
+    qkv_across = pair_step(*qkv_state, 0)
     residual = tok_buf[me_t].astype(f32)
     normed_one, inv_one = normalize(residual)
     back_one = reduce_finish(part_four, recv_four, near_four, second_four)
@@ -868,6 +959,8 @@
     for shift in range(1, groups):
         peer = lax.rem(me_d + shift, groups)
         gain_copies.append(send(gain_send.at[peer], gain_recv.at[me_d], "dp", peer))
+    for number in range(1, outer):
+        qkv_across += pair_step(*qkv_state, number)
     mlp_grad_ref[...] = total(mlp_parts, mlp_across)
     out_grad_ref[...] = total(out_parts, out_across)
     gain_group[me_t] = total(gain_recv, gain_copies)
@@ -877,8 +970,11 @@
         gain_copies.append(send(gain_group.at[me_t], gain_group.at[me_t], "tensor", peer))
     qkv_grad_ref[...] = total(qkv_parts, qkv_across)
     gain_ref[...] = total(gain_group, gain_copies)
-    for copy in sent:
-        copy.wait_send()
+    for copy, condition in sent:
+        if condition is None:
+            copy.wait_send()
+        else:
+            pl.when(condition)(copy.wait_send)
 
 
 def rotary_table(row_count):
@@ -942,7 +1038,9 @@
         parts, arrived, passed,
         vmem((groups, 8, 128), f32), vmem((groups, 8, 128), f32), vmem((members, 8, 128), f32),
     ]
-    gathers = 3 * (2 * outer - 1) + 4 * (2 * rings - 1)
+    cuts = 2 if block % 32 == 0 else 1
+    chains = 2 * cuts * (4 * (outer - 1) + 1)
+    gathers = 2 * outer - 1 + chains + 4 * (2 * rings - 1)
     reduces = 4 * (2 * rings - 1) + 3 * (2 * outer - 1)
     slots = gathers + reduces + groups + members - 2
     dims = (own_rows, width, block, heads_wide, hidden, pad_hidden)
@@ -972,20 +1070,68 @@
         attn_gain.reshape(1, block), mlp_gain.reshape(1, block),
         jnp.asarray(rotary_table(row_count)),
     )
-    grad_w_qkv = jnp.stack(
-        [qkv_sum[:, i * heads_wide : (i + 1) * heads_wide] for i in range(3)]
-    )
-    grad_w_in = jnp.stack([mlp_sums[:, :hidden], mlp_sums[:, hidden : 2 * hidden]])
+    results = pl.pallas_call(
+        functools.partial(finish_kernel, hidden),
+        out_shape=[
+            jax.ShapeDtypeStruct(output.shape, bf16),
+            jax.ShapeDtypeStruct(input_grad.shape, f32),
+            jax.ShapeDtypeStruct(w_qkv.shape, f32),
+            jax.ShapeDtypeStruct(w_out.shape, f32),
+            jax.ShapeDtypeStruct(w_in.shape, f32),
+            jax.ShapeDtypeStruct(w_down.shape, f32),
+        ],
+        in_specs=[pl.BlockSpec(memory_space=pltpu.VMEM)] * 5,
+        out_specs=[pl.BlockSpec(memory_space=pl.ANY)] * 6,
+        scratch_shapes=[
+            vmem(w_qkv.shape, f32),
+            vmem(w_out.shape, f32),
+            vmem(w_in.shape, f32),
+            vmem(w_down.shape, f32),
+            pltpu.SemaphoreType.DMA((6,)),
+        ],
+        compiler_params=pltpu.CompilerParams(vmem_limit_bytes=16 << 20),
+    )(output, input_grad, qkv_sum, out_sum, mlp_sums)
+    output, input_grad, grad_w_qkv, grad_w_out, grad_w_in, grad_w_down = results
     return (
         output,
         input_grad,
         gains[0, :block],
         grad_w_qkv,
-        out_sum.T,
+        grad_w_out,
         gains[1, :block],
         grad_w_in,
-        mlp_sums[:, 2 * hidden : 3 * hidden].T,
-    )
+        grad_w_down,
+    )
+
+
+def finish_kernel(hidden, *refs):
+    (
+        output, input_grad, qkv_sum, out_sum, mlp_sums,
+        output_to, input_grad_to, qkv_to, out_to, up_to, down_to,
+        qkv_buf, out_buf, up_buf, down_buf, sems,
+    ) = refs
+    started = []
+
+    def put(source, target):
+        copy = pltpu.make_async_copy(source, target, sems.at[len(started)])
+        copy.start()
+        started.append(copy)
+
+    put(output, output_to)
+    put(input_grad, input_grad_to)
+    heads_wide = out_sum.shape[1]
+    for which in range(3):
+        qkv_buf[which] = qkv_sum[:, which * heads_wide : (which + 1) * heads_wide]
+    put(qkv_buf, qkv_to)
+    for which in range(2):
+        up_buf[which] = mlp_sums[:, which * hidden : (which + 1) * hidden]
+    put(up_buf, up_to)
+    out_buf[...] = jnp.transpose(out_sum[...])
+    put(out_buf, out_to)
+    down_buf[...] = jnp.transpose(mlp_sums[:, 2 * hidden : 3 * hidden])
+    put(down_buf, down_to)
+    for copy in started:
+        copy.wait()
 
 
 def fits_whole(sizes, tokens, w_qkv):

time: 116 us -> 98.2 us (0.85)
  the two profiles are of different devices: /device:TPU:27 before, /device:TPU:0 now
where the time goes in v2:
time: 98.2 us; the launch traced here: 97.9 us
  Pallas kernels  91 us (93%)
  local copies, waits for them, and re-layouts  6.01 us (6%)
    pallas_call x1, Pallas kernels, whole_layer(): pl.pallas_call(functools.partial(layer_kernel, sizes, dims), out_shape=[j...  89.9 us
    unnamed x10, local copies, waits for them, and re-layouts  4.74 us

profile of v2, /device:TPU:0, one launch (start us, length us, event | category | flops | bytes accessed | tf_op | source)
XLA Modules:
  0.0 97.9 jit_solution(8373342891004874288)
XLA Ops:
  0.6 89.9 %shard_map.152 = (bf16[128,768]{1,0:T(8,128)(2,1)}, f32[128,768]{1,0:T(8,128)}, f32[8,128]{1,0:T(8,128)}, f32[96,576]{1,0:T(8,128)}, f32[96,192]{1,0:T(8,128)}, /*index=5*/f32[96,896]{1,0:T(8,128)}) custom-call(bf16[128,768]{1,0:T(8,128)(2,1)} %refs_0_.1, bf16[128,768]{1,0:T(8,128)(2,1)} %refs_1_.1, bf16[3,96,192]{2,1,0:T(8,128)(2,1)} %refs_2_.1, ...), custom_call_target="tpu_custom_call" | custom-call | tf_op jit(solution)/shard_map/pallas_call | solution.py:1047
  90.5 1.3 %slice_bitcast_fusion = (f32[96]{0:T(128)}, f32[96]{0:T(128)}) fusion(f32[8,128]{1,0:T(8,128)} %get-tuple-element.27), kind=kLoop, calls=%fused_computation | loop fusion | bytes 1536 | tf_op jit(solution)/shard_map/squeeze | solution.py:1101
  91.8 0.0 copy-start
  91.8 1.0 %copy-done = f32[128,768]{1,0:T(8,128)S(1)} copy-done((f32[128,768]{1,0:T(8,128)S(1)}, f32[128,768]{1,0:T(8,128)}, u32[]{:S(2)}) %copy-start) | copy-done | bytes 393240
  92.8 0.0 copy-start.1
  92.8 1.0 copy-done.1
  93.8 0.0 copy-start.2
  93.8 0.9 copy-done.2
  94.7 0.0 copy-start.3
  94.7 0.9 copy-done.3
  95.7 0.0 copy-start.4
  95.7 0.9 copy-done.4
  96.6 1.1 %shard_map.153 = (bf16[128,768]{1,0:T(8,128)(2,1)}, f32[128,768]{1,0:T(8,128)}, f32[3,96,192]{2,1,0:T(8,128)}, f32[192,96]{1,0:T(8,128)}, f32[2,96,288]{2,1,0:T(8,128)}, /*index=5*/f32[288,96]{1,0:T(8,128)}) custom-call(bf16[128,768]{1,0:T(8,128)(2,1)S(1)} %copy-done.3, f32[128,768]{1,0:T(8,128)S(1)} %copy-done, f32[96,576]{1,0:T(8,128)S(1)} %copy-done.2, ...), custom_call_target="tpu_custom_call" | custom-call | tf_op jit(solution)/shard_map/pallas_call | solution.py:1073
Async XLA Ops:
  91.8 1.0 %copy-start = (f32[128,768]{1,0:T(8,128)S(1)}, f32[128,768]{1,0:T(8,128)}, u32[]{:S(2)}) copy-start(f32[128,768]{1,0:T(8,128)} %get-tuple-element.21.refs_1_) | copy-start | bytes 1179652
  92.8 1.0 copy-start.1
  93.8 0.9 copy-start.2
  94.7 0.9 copy-start.3
  95.7 0.9 copy-start.4

commit v3 on v2

--- a/solution.py
+++ b/solution.py
@@ -645,20 +645,22 @@
         mirrored = origin // 2 * 2 + 1 - col
         return (send(buffer.at[origin], buffer.at[origin], "dp", x_peer), mirrored)
 
-    def tensor_spread(buffer):
+    def tensor_spread(buffer, span=slice(0, own_rows)):
         copies = []
+        own = buffer.at[me_t, span]
         for shift in range(1, rings):
             peer = lax.rem(yrow + shift, rings) * 2 + core
             origin = lax.rem(yrow + rings - shift, rings) * 2 + core
-            copies.append((send(buffer.at[me_t], buffer.at[me_t], "tensor", peer), origin))
-        near = send(buffer.at[me_t], buffer.at[me_t], "tensor", c_peer)
+            copies.append((send(own, own, "tensor", peer), origin))
+        near = send(own, own, "tensor", c_peer)
         return copies, near
 
-    def tensor_relay(buffer, copies):
+    def tensor_relay(buffer, copies, span=slice(0, own_rows)):
         onward = []
         for copy, origin in copies:
             copy.wait_recv()
-            onward.append(send(buffer.at[origin], buffer.at[origin], "tensor", c_peer))
+            piece = buffer.at[origin, span]
+            onward.append(send(piece, piece, "tensor", c_peer))
         return onward
 
     gain_z = dp_spread(gain_buf)
@@ -751,52 +753,88 @@
         mix[:, :, head * 128 : (head + 1) * 128] = mixed.reshape(members, own_rows, 128)
         mix_pack[:, head * HD : (head + 1) * HD] = mixed[:, :HD]
 
-    def reduce_start(part, recv):
+    every = slice(0, own_rows)
+    if own_rows % 32 == 0:
+        spans = (slice(0, own_rows // 2), slice(own_rows // 2, own_rows))
+    else:
+        spans = (every,)
+
+    def reduce_far(part, recv, span=every):
         first = []
         for shift in range(1, rings):
             far = lax.rem(yrow + shift, rings)
-            first.append(send(part.at[far * 2 + 1 - core], recv.at[shift], "tensor", c_peer))
-        return first, send(part.at[c_peer], recv.at[0], "tensor", c_peer)
-
-    def reduce_middle(part, recv, fwd, first):
+            first.append(
+                send(part.at[far * 2 + 1 - core, span], recv.at[shift, span], "tensor", c_peer)
+            )
+        return first
+
+    def reduce_near(part, recv, span=every):
+        return send(part.at[c_peer, span], recv.at[0, span], "tensor", c_peer)
+
+    def reduce_middle(part, recv, fwd, first, span=every):
         second = []
         for shift in range(1, rings):
             far = lax.rem(yrow + shift, rings)
             first[shift - 1].wait_recv()
-            fwd[shift] = (part[far * 2 + core].astype(f32) + recv[shift].astype(f32)).astype(bf16)
+            fwd[shift, span] = (
+                part[far * 2 + core, span].astype(f32) + recv[shift, span].astype(f32)
+            ).astype(bf16)
             second.append(
-                send(fwd.at[shift], recv.at[rings + shift], "tensor", far * 2 + core)
+                send(
+                    fwd.at[shift, span],
+                    recv.at[rings + shift, span],
+                    "tensor",
+                    far * 2 + core,
+                )
             )
         return second
 
-    def reduce_finish(part, recv, near, second):
+    def reduce_finish(part, recv, near, second, span=every):
         near.wait_recv()
-        total = part[me_t].astype(f32) + recv[0].astype(f32)
+        total = part[me_t, span].astype(f32) + recv[0, span].astype(f32)
         for shift in range(1, rings):
             second[shift - 1].wait_recv()
-            total = total + recv[rings + shift].astype(f32)
+            total = total + recv[rings + shift, span].astype(f32)
         return total
 
+    def project(part, ring, left, right):
+        part[pl.ds(2 * ring, 2)] = (
+            dot_f32(left, right, 1, 1).astype(bf16).reshape(2, own_rows, width)
+        )
+
     out_weight = w_out_pad[...].reshape(width, spread)
-    part_one[...] = (
-        dot_f32(mix[...].reshape(row_count, spread), out_weight, 1, 1)
-        .astype(bf16)
-        .reshape(members, own_rows, width)
-    )
-    first_one, near_one = reduce_start(part_one, recv_one)
-    second_one = reduce_middle(part_one, recv_one, fwd_one, first_one)
+
+    def mixed_ring(ring):
+        return mix[pl.ds(2 * ring, 2)].reshape(2 * own_rows, spread)
+
+    for shift in range(1, rings):
+        far = lax.rem(yrow + shift, rings)
+        project(part_one, far, mixed_ring(far), out_weight)
+    first_one = [reduce_far(part_one, recv_one, span) for span in spans]
+    project(part_one, yrow, mixed_ring(yrow), out_weight)
+    near_one = [reduce_near(part_one, recv_one, span) for span in spans]
+    second_one = [
+        reduce_middle(part_one, recv_one, fwd_one, first, span)
+        for first, span in zip(first_one, spans)
+    ]
     for number in range(2, outer - 1):
         chain_b.step(number)
     for head in range(head_count):
         q_buf[head] = dot_f32(q_buf[head], paired, 1, 0).astype(bf16)
         k_buf[head] = dot_f32(k_buf[head], paired, 1, 0).astype(bf16)
-    residual = tok_buf[me_t].astype(f32)
-    hidden_res[...] = residual + reduce_finish(part_one, recv_one, near_one, second_one)
-    normed_two, inv_two = normalize(hidden_res[...])
-    rows_two[me_t] = (normed_two * mlp_gain).astype(bf16)
-    rows_y, rows_near = tensor_spread(rows_two)
     if outer > 2:
         chain_b.step(outer - 1)
+    rows_y, rows_near = [], []
+    for index, span in enumerate(spans):
+        residual = tok_buf[me_t, span].astype(f32)
+        hidden_res[span] = residual + reduce_finish(
+            part_one, recv_one, near_one[index], second_one[index], span
+        )
+        normed_two = normalize(hidden_res[span])[0]
+        rows_two[me_t, span] = (normed_two * mlp_gain).astype(bf16)
+        far_copies, near_copy = tensor_spread(rows_two, span)
+        rows_y.append(far_copies)
+        rows_near.append(near_copy)
     cot_near.wait_recv()
     for copy in cot_far:
         copy.wait_recv()
@@ -828,19 +866,24 @@
             .reshape(2, own_rows, width)
         )
 
-    rows_near.wait_recv()
-    rows_far = tensor_relay(rows_two, rows_y)
+    for copy in rows_near:
+        copy.wait_recv()
     feed(yrow)
+    rows_far = []
+    for copies, span in zip(rows_y, spans):
+        rows_far += tensor_relay(rows_two, copies, span)
     for copy in rows_far:
         copy.wait_recv()
     for shift in range(1, rings):
         feed(lax.rem(yrow + shift, rings))
-    first_two, near_two = reduce_start(part_two, recv_two)
-    second_two = reduce_middle(part_two, recv_two, fwd_two, first_two)
+    first_two = reduce_far(part_two, recv_two)
+    near_two = reduce_near(part_two, recv_two)
+
+    shifts = sorted(range(1, outer), key=lambda shift: abs(shift - outer // 2)) + [outer]
 
     def pair_start(grads, half):
         copies = []
-        for shift in range(1, outer + 1):
+        for shift in shifts:
             row = lax.rem(zrow + shift, outer)
             copies.append((send(grads.at[row * 2 + 1 - col], half.at[row], "dp", x_peer), row))
         return copies
@@ -872,6 +915,7 @@
             (groups, block, pad_hidden - 3 * hidden), bf16
         )
     mlp_pairs = pair_start(mlp_grads, mlp_half)
+    second_two = reduce_middle(part_two, recv_two, fwd_two, first_two)
     part_three[...] = (
         dot_f32(full_act, down_w[...], 1, 1).astype(bf16).reshape(members, own_rows, width)
     )
@@ -881,9 +925,12 @@
     grad_hidden[...] = cot_buf[me_t].astype(f32) + grad_res
     grad_rows[me_t] = grad_hidden[...].astype(bf16)
     grad_y, grad_near = tensor_spread(grad_rows)
-    first_three, near_three = reduce_start(part_three, recv_three)
+    first_three = reduce_far(part_three, recv_three)
+    near_three = reduce_near(part_three, recv_three)
     mlp_state = (mlp_grads, mlp_half, mlp_sum, mlp_parts, mlp_pairs)
     mlp_across = pair_step(*mlp_state, 0)
+    for number in range(1, min(2, outer - 1)):
+        mlp_across += pair_step(*mlp_state, number)
     grad_far = tensor_relay(grad_rows, grad_y)
     second_three = reduce_middle(part_three, recv_three, fwd_three, first_three)
     grad_near.wait_recv()
@@ -895,7 +942,7 @@
         dot_f32(full_grad, mix_pack[...], 0, 0).astype(bf16).reshape(groups, block, heads_wide)
     )
     out_pairs = pair_start(out_grads, out_half)
-    for number in range(1, outer - 2):
+    for number in range(2, outer - 1):
         mlp_across += pair_step(*mlp_state, number)
     scale = HD ** (-0.5)
     for head in range(head_count):
@@ -920,12 +967,16 @@
     )
     qkv_pairs = pair_start(qkv_grads, qkv_half)
     qkv_weight = w_a[:, :, : 3 * heads_wide].reshape(width, 3 * heads_wide)
-    part_four[...] = (
-        dot_f32(proj_grad[...], qkv_weight, 1, 1)
-        .astype(bf16)
-        .reshape(members, own_rows, width)
-    )
-    first_four, near_four = reduce_start(part_four, recv_four)
+
+    def grad_ring(ring):
+        return proj_grad[pl.ds(pl.multiple_of(ring * 2 * own_rows, 2 * own_rows), 2 * own_rows)]
+
+    for shift in range(1, rings):
+        far = lax.rem(yrow + shift, rings)
+        project(part_four, far, grad_ring(far), qkv_weight)
+    first_four = reduce_far(part_four, recv_four)
+    project(part_four, yrow, grad_ring(yrow), qkv_weight)
+    near_four = reduce_near(part_four, recv_four)
     second_four = reduce_middle(part_four, recv_four, fwd_four, first_four)
 
     def total(parts, across):
@@ -933,16 +984,13 @@
             copy.wait_recv()
         return jnp.sum(parts[...].astype(f32), axis=0)
 
-    for number in range(max(outer - 2, 1), outer):
-        mlp_across += pair_step(*mlp_state, number)
+    mlp_across += pair_step(*mlp_state, outer - 1)
     mlp_out = reduce_finish(part_three, recv_three, near_three, second_three)
     output_ref[...] = (hidden_res[...] + mlp_out).astype(bf16)
     out_state = (out_grads, out_half, out_sum, out_parts, out_pairs)
     out_across = []
     for number in range(outer):
         out_across += pair_step(*out_state, number)
-    qkv_state = (qkv_grads, qkv_half, qkv_sum, qkv_parts, qkv_pairs)
-    qkv_across = pair_step(*qkv_state, 0)
     residual = tok_buf[me_t].astype(f32)
     normed_one, inv_one = normalize(residual)
     back_one = reduce_finish(part_four, recv_four, near_four, second_four)
@@ -959,17 +1007,20 @@
     for shift in range(1, groups):
         peer = lax.rem(me_d + shift, groups)
         gain_copies.append(send(gain_send.at[peer], gain_recv.at[me_d], "dp", peer))
-    for number in range(1, outer):
+    mlp_grad_ref[...] = total(mlp_parts, mlp_across)
+    qkv_state = (qkv_grads, qkv_half, qkv_sum, qkv_parts, qkv_pairs)
+    qkv_across = pair_step(*qkv_state, 0)
+    for number in range(1, outer - 1):
         qkv_across += pair_step(*qkv_state, number)
-    mlp_grad_ref[...] = total(mlp_parts, mlp_across)
-    out_grad_ref[...] = total(out_parts, out_across)
     gain_group[me_t] = total(gain_recv, gain_copies)
     gain_copies = []
     for shift in range(1, members):
         peer = lax.rem(me_t + shift, members)
         gain_copies.append(send(gain_group.at[me_t], gain_group.at[me_t], "tensor", peer))
+    out_grad_ref[...] = total(out_parts, out_across)
+    qkv_across += pair_step(*qkv_state, outer - 1)
+    gain_ref[...] = total(gain_group, gain_copies)
     qkv_grad_ref[...] = total(qkv_parts, qkv_across)
-    gain_ref[...] = total(gain_group, gain_copies)
     for copy, condition in sent:
         if condition is None:
             copy.wait_send()
@@ -1040,8 +1091,9 @@
     ]
     cuts = 2 if block % 32 == 0 else 1
     chains = 2 * cuts * (4 * (outer - 1) + 1)
-    gathers = 2 * outer - 1 + chains + 4 * (2 * rings - 1)
-    reduces = 4 * (2 * rings - 1) + 3 * (2 * outer - 1)
+    halves = 2 if own_rows % 32 == 0 else 1
+    gathers = 2 * outer - 1 + chains + (3 + halves) * (2 * rings - 1)
+    reduces = (3 + halves) * (2 * rings - 1) + 3 * (2 * outer - 1)
     slots = gathers + reduces + groups + members - 2
     dims = (own_rows, width, block, heads_wide, hidden, pad_hidden)
     output, input_grad, gains, qkv_sum, out_sum, mlp_sums = pl.pallas_call(
@@ -1054,7 +1106,7 @@
             jax.ShapeDtypeStruct((block, heads_wide), f32),
             jax.ShapeDtypeStruct((block, pad_hidden), f32),
         ],
-        in_specs=[pl.BlockSpec(memory_space=pl.ANY)] * 9,
+        in_specs=[pl.BlockSpec(memory_space=pltpu.HBM)] * 9,
         out_specs=[pl.BlockSpec(memory_space=pltpu.VMEM)] * 6,
         scratch_shapes=scratch
         + [
@@ -1063,12 +1115,17 @@
             pltpu.SemaphoreType.DMA((slots,)),
         ],
         compiler_params=pltpu.CompilerParams(
-            collective_id=0, has_side_effects=True, vmem_limit_bytes=60 << 20
+            collective_id=0, has_side_effects=True, vmem_limit_bytes=44 << 20
         ),
     )(
-        tokens, cotangent, w_qkv, w_out, w_in, w_down,
-        attn_gain.reshape(1, block), mlp_gain.reshape(1, block),
-        jnp.asarray(rotary_table(row_count)),
+        *[
+            pltpu.with_memory_space_constraint(array, pltpu.HBM)
+            for array in (
+                tokens, cotangent, w_qkv, w_out, w_in, w_down,
+                attn_gain.reshape(1, block), mlp_gain.reshape(1, block),
+                jnp.asarray(rotary_table(row_count)),
+            )
+        ]
     )
     results = pl.pallas_call(
         functools.partial(finish_kernel, hidden),
@@ -1079,26 +1136,30 @@
             jax.ShapeDtypeStruct(w_out.shape, f32),
             jax.ShapeDtypeStruct(w_in.shape, f32),
             jax.ShapeDtypeStruct(w_down.shape, f32),
+            jax.ShapeDtypeStruct((1, block), f32),
+            jax.ShapeDtypeStruct((1, block), f32),
         ],
-        in_specs=[pl.BlockSpec(memory_space=pltpu.VMEM)] * 5,
-        out_specs=[pl.BlockSpec(memory_space=pl.ANY)] * 6,
+        in_specs=[pl.BlockSpec(memory_space=pltpu.VMEM)] * 6,
+        out_specs=[pl.BlockSpec(memory_space=pltpu.HBM)] * 8,
         scratch_shapes=[
             vmem(w_qkv.shape, f32),
             vmem(w_out.shape, f32),
             vmem(w_in.shape, f32),
             vmem(w_down.shape, f32),
-            pltpu.SemaphoreType.DMA((6,)),
+            vmem((1, block), f32),
+            vmem((1, block), f32),
+            pltpu.SemaphoreType.DMA((8,)),
         ],
         compiler_params=pltpu.CompilerParams(vmem_limit_bytes=16 << 20),
-    )(output, input_grad, qkv_sum, out_sum, mlp_sums)
-    output, input_grad, grad_w_qkv, grad_w_out, grad_w_in, grad_w_down = results
+    )(output, input_grad, qkv_sum, out_sum, mlp_sums, gains)
+    output, input_grad, grad_w_qkv, grad_w_out, grad_w_in, grad_w_down = results[:6]
     return (
         output,
         input_grad,
-        gains[0, :block],
+        results[6].reshape(block),
         grad_w_qkv,
         grad_w_out,
-        gains[1, :block],
+        results[7].reshape(block),
         grad_w_in,
         grad_w_down,
     )
@@ -1106,9 +1167,9 @@
 
 def finish_kernel(hidden, *refs):
     (
-        output, input_grad, qkv_sum, out_sum, mlp_sums,
-        output_to, input_grad_to, qkv_to, out_to, up_to, down_to,
-        qkv_buf, out_buf, up_buf, down_buf, sems,
+        output, input_grad, qkv_sum, out_sum, mlp_sums, gains,
+        output_to, input_grad_to, qkv_to, out_to, up_to, down_to, attn_to, mlp_to,
+        qkv_buf, out_buf, up_buf, down_buf, attn_buf, mlp_buf, sems,
     ) = refs
     started = []
 
@@ -1119,6 +1180,10 @@
 
     put(output, output_to)
     put(input_grad, input_grad_to)
+    attn_buf[...] = gains[0:1, : attn_buf.shape[1]]
+    put(attn_buf, attn_to)
+    mlp_buf[...] = gains[1:2, : mlp_buf.shape[1]]
+    put(mlp_buf, mlp_to)
     heads_wide = out_sum.shape[1]
     for which in range(3):
         qkv_buf[which] = qkv_sum[:, which * heads_wide : (which + 1) * heads_wide]

time: 98.2 us -> 86.1 us (0.88)
  local copies, waits for them, and re-layouts: 6.01 us -> 0 us
  Pallas kernels: 91 us -> 85.1 us
    pallas_call x1, Pallas kernels: 89.9 us -> 84 us  [whole_layer(): pl.pallas_call(functools.partial(layer_kernel, sizes, dims), out_shape=[j...]
    unnamed x10 -> x0, local copies, waits for them, and re-layouts: 4.74 us -> none
    squeeze x1 -> x0, local copies, waits for them, and re-layouts: 1.28 us -> none  [whole_layer(): gains[1, :block]]
where the time goes in v3:
time: 86.1 us; the launch traced here: 85.9 us
  Pallas kernels  85.1 us (99%)
    pallas_call x1, Pallas kernels, whole_layer(): pl.pallas_call(functools.partial(layer_kernel, sizes, dims), out_shape=[j...  84 us

profile of v3, /device:TPU:0, one launch (start us, length us, event | category | flops | bytes accessed | tf_op | source)
XLA Modules:
  0.0 85.9 jit_solution(13843020047025710348)
XLA Ops:
  0.6 84.0 %shard_map.152 = (bf16[128,768]{1,0:T(8,128)(2,1)S(1)}, f32[128,768]{1,0:T(8,128)S(1)}, f32[8,128]{1,0:T(8,128)S(1)}, f32[96,576]{1,0:T(8,128)S(1)}, f32[96,192]{1,0:T(8,128)S(1)}, /*index=5*/f32[96,896]{1,0:T(8,128)S(1)}) custom-call(bf16[128,768]{1,0:T(8,128)(2,1)} %refs_0_.1, bf16[128,768]{1,0:T(8,128)(2,1)} %refs_1_.1, bf16[3,96,192]{2,1,0:T(8,128)(2,1)} %refs_2_.1, ...), custom_call_target="tpu_custom_call" | custom-call | tf_op jit(solution)/shard_map/pallas_call | solution.py:1099
  84.6 1.2 %shard_map.153 = (bf16[128,768]{1,0:T(8,128)(2,1)}, f32[128,768]{1,0:T(8,128)}, f32[3,96,192]{2,1,0:T(8,128)}, f32[192,96]{1,0:T(8,128)}, f32[2,96,288]{2,1,0:T(...) custom-call(bf16[128,768]{1,0:T(8,128)(2,1)S(1)} %get-tuple-element.22.refs_0_, ...), custom_call_target="tpu_custom_call" | custom-call | tf_op jit(solution)/shard_map/pallas_call | solution.py:1130

commit v4 on v3

--- a/solution.py
+++ b/solution.py
@@ -484,20 +484,22 @@
     own_rows, width, block, heads_wide, hidden, pad_hidden = dims
     head_count = heads_wide // HD
     spread = 2 * heads_wide
+    side = -3 * heads_wide % 128
     row_count = own_rows * members
     outer, rings = groups // 2, members // 2
     (
         tok_in, cot_in, qkv_in, out_in, up_in, down_in, attn_in, mlp_in, table_in,
         output_ref, input_grad_ref, gain_ref, qkv_grad_ref, out_grad_ref, mlp_grad_ref,
         tok_buf, cot_buf, qkv_raw, out_raw, up_raw, down_raw, attn_raw, mlp_raw, table,
-        w_a, w_b, gain_buf, gain_rows, w_big, w_out_pad, up_w, gate_w, down_w,
+        w_a, w_b, w_c, gain_buf, gain_rows, w_big, w_out_pad, up_w, gate_w, down_w,
         rows_one, probs, q_buf, k_buf, v_buf, mix_t, mix, mix_pack,
         part_one, recv_one, fwd_one, hidden_res, rows_two,
         act_buf, up_grad, gate_grad, part_two, recv_two, fwd_two,
         part_three, recv_three, fwd_three,
         mlp_grads, mlp_half, mlp_sum, mlp_parts,
         grad_hidden, grad_rows, out_grads, out_half, out_sum, out_parts,
-        proj_grad, qkv_grads, qkv_half, qkv_sum, qkv_parts,
+        proj_grad, qk_grads, qk_half, qk_sum, qk_parts,
+        vo_grads, vo_half, vo_sum, vo_parts,
         part_four, recv_four, fwd_four, gain_send, gain_recv, gain_group,
         load_sem, send_sem, recv_sem,
     ) = refs
@@ -540,20 +542,20 @@
             self.moves = {}
             last = outer - 1
             for step in range(1, outer):
-                for side in (0, 1):
-                    ahead = 1 if side == 0 else outer - 1
+                for way in (0, 1):
+                    ahead = 1 if way == 0 else outer - 1
                     target = lax.rem(zrow + ahead, outer) * 2 + col
-                    back = step - 1 if side else outer - step + 1
+                    back = step - 1 if way else outer - step + 1
                     carried = lax.rem(zrow + back, outer) * 2 + col
-                    origin = lax.rem(zrow + (step if side else outer - step), outer) * 2
-                    lands = zrow + step <= last if side else zrow >= step
+                    origin = lax.rem(zrow + (step if way else outer - step), outer) * 2
+                    lands = zrow + step <= last if way else zrow >= step
                     starts = (
                         (zrow >= 1) & (zrow + step - 1 <= last)
-                        if side
+                        if way
                         else (zrow < last) & (zrow >= step - 1)
                     )
                     for cut in range(cuts):
-                        self.moves[step, side, cut] = (
+                        self.moves[step, way, cut] = (
                             make(self.piece(carried, cut), self.piece(carried, cut), "dp", target),
                             make(
                                 self.piece(origin + col, cut),
@@ -570,32 +572,35 @@
             return self.buffer.at[index, cut * height : (cut + 1) * height]
 
         def start(self):
+            for cut in range(cuts):
+                for way in (0, 1):
+                    move, _, starts, _, _ = self.moves[1, way, cut]
+                    begin(move, starts)
+
+        def start_pair(self):
             self.own = []
             for cut in range(cuts):
-                for side in (0, 1):
-                    move, _, starts, _, _ = self.moves[1, side, cut]
-                    begin(move, starts)
                 piece = self.piece(me_d, cut)
                 self.own.append(send(piece, piece, "dp", x_peer))
 
         def step(self, number):
             for cut in range(cuts):
-                for side in (0, 1):
-                    move, across, _, lands, _ = self.moves[number, side, cut]
+                for way in (0, 1):
+                    move, across, _, lands, _ = self.moves[number, way, cut]
                     pl.when(lands)(move.wait_recv)
                     if number + 1 < outer:
-                        onward, _, starts, _, _ = self.moves[number + 1, side, cut]
+                        onward, _, starts, _, _ = self.moves[number + 1, way, cut]
                         begin(onward, starts)
                     begin(across, lands)
 
         def paired(self, number, then=None):
-            for side in (0, 1):
-                lands, origin = self.moves[number, side, 0][3:]
+            for way in (0, 1):
+                lands, origin = self.moves[number, way, 0][3:]
 
                 @pl.when(lands)
                 def _():
                     for cut in range(cuts):
-                        self.moves[number, side, cut][1].wait_recv()
+                        self.moves[number, way, cut][1].wait_recv()
                     if then is not None:
                         then(origin + 1 - col)
 
@@ -630,7 +635,10 @@
     gain_buf[me_d, 8:9, :block] = mlp_raw[...]
     for which in range(3):
         w_a[me_d, :, which * heads_wide : (which + 1) * heads_wide] = qkv_raw[which]
-    w_a[me_d, :, 3 * heads_wide :] = dot_f32(out_raw[...], eye_heads, 0, 0).astype(bf16)
+    out_turned = dot_f32(out_raw[...], eye_heads, 0, 0).astype(bf16)
+    if side:
+        w_a[me_d, :, 3 * heads_wide :] = out_turned[:, :side]
+    w_c[me_d] = out_turned[:, side:]
     pl.semaphore_wait(barrier, groups + members - 2)
 
     def dp_spread(buffer):
@@ -667,6 +675,7 @@
     gain_x = [dp_pair(gain_buf, me_d)]
     chain_a = Chain(w_a)
     chain_a.start()
+    chain_a.start_pair()
     for load in loads[4:6]:
         load.wait()
     tok_y, tok_near = tensor_spread(tok_buf)
@@ -692,8 +701,15 @@
             w_big[index, :, which * spread : (which + 1) * spread] = dot_f32(
                 piece, matrix, 1, 0
             ).astype(bf16)
-        piece = w_a[index, :, 3 * heads_wide :]
-        w_out_pad[index] = dot_f32(piece, plain, 1, 0).astype(bf16)
+
+    def expand_out():
+        value = dot_f32(
+            w_c[...].reshape(width, heads_wide - side), plain[side:], 1, 0
+        )
+        if side:
+            head_piece = w_a[:, :, 3 * heads_wide :].reshape(width, side)
+            value = value + dot_f32(head_piece, plain[:side], 1, 0)
+        w_out_pad[...] = value.astype(bf16).reshape(groups, block, spread)
 
     expand(me_d)
     chain_a.step(1)
@@ -703,6 +719,8 @@
     tok_far = tensor_relay(tok_buf, tok_y)
     for number in range(2, outer - 1):
         chain_a.step(number)
+    c_z = dp_spread(w_c)
+    chain_b.start()
     for copy, _ in gain_x:
         copy.wait_recv()
     for index in range(groups):
@@ -717,13 +735,18 @@
     rows_one[...] = (normalize(all_rows)[0] * attn_gain).astype(bf16)
     if outer > 2:
         chain_a.step(outer - 1)
-    chain_b.start()
+    c_x = [dp_pair(w_c, me_d)]
     cot_far = tensor_relay(cot_buf, cot_y)
     for shift in range(1, outer):
         expand(lax.rem(zrow + shift, outer) * 2 + col)
+    for copy, origin in c_z:
+        copy.wait_recv()
+        c_x.append(dp_pair(w_c, origin))
+    chain_b.start_pair()
     for copy in chain_a.own:
         copy.wait_recv()
     expand(x_peer)
+    chain_b.step(1)
     for number in range(1, outer):
         chain_a.paired(number, expand)
 
@@ -740,7 +763,6 @@
             turned = piece * rotary
             turned = (turned + pltpu.roll(turned, 64, 1)).astype(bf16)
             (q_buf, k_buf)[which][head] = turned
-    chain_b.step(1)
     for head in range(head_count):
         scores = dot_f32(k_buf[head], q_buf[head], 1, 1) * (0.5 * HD ** (-0.5))
         peak = jnp.max(scores, axis=0, keepdims=True)
@@ -802,6 +824,9 @@
             dot_f32(left, right, 1, 1).astype(bf16).reshape(2, own_rows, width)
         )
 
+    for copy, _ in c_x:
+        copy.wait_recv()
+    expand_out()
     out_weight = w_out_pad[...].reshape(width, spread)
 
     def mixed_ring(ring):
@@ -879,24 +904,43 @@
     first_two = reduce_far(part_two, recv_two)
     near_two = reduce_near(part_two, recv_two)
 
-    shifts = sorted(range(1, outer), key=lambda shift: abs(shift - outer // 2)) + [outer]
+    staged = outer == 4
+    beside = zrow // 2 * 2 + 1 - lax.rem(zrow, 2)
+    if staged:
+        across_z = lax.rem(zrow + 2, outer)
+        targets = [lax.rem(beside + 2, outer), across_z, beside, zrow]
+    else:
+        targets = [lax.rem(zrow + shift, outer) for shift in range(1, outer + 1)]
 
     def pair_start(grads, half):
-        copies = []
-        for shift in shifts:
-            row = lax.rem(zrow + shift, outer)
-            copies.append((send(grads.at[row * 2 + 1 - col], half.at[row], "dp", x_peer), row))
-        return copies
-
-    def pair_step(grads, half, sums, parts, copies, number):
+        return [
+            (send(grads.at[row * 2 + 1 - col], half.at[row], "dp", x_peer), row)
+            for row in targets
+        ]
+
+    def pair_step(state, number):
+        grads, half, sums, parts, copies, moved = state
         copy, row = copies[number]
         copy.wait_recv()
-        value = (grads[row * 2 + col].astype(f32) + half[row].astype(f32)).astype(bf16)
+        value = grads[row * 2 + col].astype(f32) + half[row].astype(f32)
         if number == outer - 1:
-            parts[row] = value
-            return []
-        sums[row] = value
-        return [send(sums.at[row], parts.at[zrow], "dp", row * 2 + col)]
+            for copy in moved[1:] if staged else moved:
+                copy.wait_recv()
+            if not staged:
+                parts[zrow] = jnp.zeros(parts.shape[1:], bf16)
+            arrived = parts[1 : outer - 1] if staged else parts[...]
+            return value + jnp.sum(arrived.astype(f32), axis=0)
+        if not staged:
+            sums[row] = value.astype(bf16)
+            moved.append(send(sums.at[row], parts.at[zrow], "dp", row * 2 + col))
+            return None
+        if number == 1:
+            moved[0].wait_recv()
+            value = value + parts[0].astype(f32)
+        sums[number] = value.astype(bf16)
+        target, place = ((beside, 0), (across_z, 1), (beside, 2))[number]
+        moved.append(send(sums.at[number], parts.at[place], "dp", target * 2 + col))
+        return None
 
     full_rows = rows_two[...].reshape(row_count, width)
     full_cot = cot_buf[...].reshape(row_count, width)
@@ -920,6 +964,8 @@
         dot_f32(full_act, down_w[...], 1, 1).astype(bf16).reshape(members, own_rows, width)
     )
     normed_two, inv_two = normalize(hidden_res[...])
+    mlp_state = (mlp_grads, mlp_half, mlp_sum, mlp_parts, mlp_pairs, [])
+    pair_step(mlp_state, 0)
     back_two = reduce_finish(part_two, recv_two, near_two, second_two)
     grad_res, mlp_gain_part = normalize_back(back_two, normed_two, inv_two, mlp_gain)
     grad_hidden[...] = cot_buf[me_t].astype(f32) + grad_res
@@ -927,10 +973,8 @@
     grad_y, grad_near = tensor_spread(grad_rows)
     first_three = reduce_far(part_three, recv_three)
     near_three = reduce_near(part_three, recv_three)
-    mlp_state = (mlp_grads, mlp_half, mlp_sum, mlp_parts, mlp_pairs)
-    mlp_across = pair_step(*mlp_state, 0)
     for number in range(1, min(2, outer - 1)):
-        mlp_across += pair_step(*mlp_state, number)
+        pair_step(mlp_state, number)
     grad_far = tensor_relay(grad_rows, grad_y)
     second_three = reduce_middle(part_three, recv_three, fwd_three, first_three)
     grad_near.wait_recv()
@@ -938,12 +982,13 @@
         copy.wait_recv()
     full_grad = grad_rows[...].reshape(row_count, width)
     grad_mix = dot_f32(full_grad, out_weight, 1, 0).astype(bf16)
-    out_grads[...] = (
-        dot_f32(full_grad, mix_pack[...], 0, 0).astype(bf16).reshape(groups, block, heads_wide)
-    )
+    out_product = dot_f32(full_grad, mix_pack[...], 0, 0).astype(bf16)
+    if side:
+        vo_grads[:, :, heads_wide:] = out_product[:, :side].reshape(groups, block, side)
+    out_grads[...] = out_product[:, side:].reshape(groups, block, heads_wide - side)
     out_pairs = pair_start(out_grads, out_half)
     for number in range(2, outer - 1):
-        mlp_across += pair_step(*mlp_state, number)
+        pair_step(mlp_state, number)
     scale = HD ** (-0.5)
     for head in range(head_count):
         grad_head = grad_mix[:, head * 128 : (head + 1) * 128]
@@ -960,12 +1005,18 @@
         for which, value in enumerate((grad_q, grad_k, grad_v)):
             start = which * heads_wide + head * HD
             proj_grad[:, start : start + HD] = value[:, :HD].astype(bf16)
-    qkv_grads[...] = (
-        dot_f32(rows_one[...], proj_grad[...], 0, 0)
+    qk_grads[...] = (
+        dot_f32(rows_one[...], proj_grad[:, : 2 * heads_wide], 0, 0)
         .astype(bf16)
-        .reshape(groups, block, 3 * heads_wide)
-    )
-    qkv_pairs = pair_start(qkv_grads, qkv_half)
+        .reshape(groups, block, 2 * heads_wide)
+    )
+    qk_pairs = pair_start(qk_grads, qk_half)
+    vo_grads[:, :, :heads_wide] = (
+        dot_f32(rows_one[...], proj_grad[:, 2 * heads_wide :], 0, 0)
+        .astype(bf16)
+        .reshape(groups, block, heads_wide)
+    )
+    vo_pairs = pair_start(vo_grads, vo_half)
     qkv_weight = w_a[:, :, : 3 * heads_wide].reshape(width, 3 * heads_wide)
 
     def grad_ring(ring):
@@ -984,13 +1035,15 @@
             copy.wait_recv()
         return jnp.sum(parts[...].astype(f32), axis=0)
 
-    mlp_across += pair_step(*mlp_state, outer - 1)
     mlp_out = reduce_finish(part_three, recv_three, near_three, second_three)
     output_ref[...] = (hidden_res[...] + mlp_out).astype(bf16)
-    out_state = (out_grads, out_half, out_sum, out_parts, out_pairs)
-    out_across = []
-    for number in range(outer):
-        out_across += pair_step(*out_state, number)
+    out_state = (out_grads, out_half, out_sum, out_parts, out_pairs, [])
+    for number in range(outer - 1):
+        pair_step(out_state, number)
+    mlp_grad_ref[...] = pair_step(mlp_state, outer - 1)
+    qk_state = (qk_grads, qk_half, qk_sum, qk_parts, qk_pairs, [])
+    vo_state = (vo_grads, vo_half, vo_sum, vo_parts, vo_pairs, [])
+    pair_step(qk_state, 0)
     residual = tok_buf[me_t].astype(f32)
     normed_one, inv_one = normalize(residual)
     back_one = reduce_finish(part_four, recv_four, near_four, second_four)
@@ -1007,20 +1060,20 @@
     for shift in range(1, groups):
         peer = lax.rem(me_d + shift, groups)
         gain_copies.append(send(gain_send.at[peer], gain_recv.at[me_d], "dp", peer))
-    mlp_grad_ref[...] = total(mlp_parts, mlp_across)
-    qkv_state = (qkv_grads, qkv_half, qkv_sum, qkv_parts, qkv_pairs)
-    qkv_across = pair_step(*qkv_state, 0)
     for number in range(1, outer - 1):
-        qkv_across += pair_step(*qkv_state, number)
+        pair_step(qk_state, number)
+    pair_step(vo_state, 0)
     gain_group[me_t] = total(gain_recv, gain_copies)
     gain_copies = []
     for shift in range(1, members):
         peer = lax.rem(me_t + shift, members)
         gain_copies.append(send(gain_group.at[me_t], gain_group.at[me_t], "tensor", peer))
-    out_grad_ref[...] = total(out_parts, out_across)
-    qkv_across += pair_step(*qkv_state, outer - 1)
+    for number in range(1, outer - 1):
+        pair_step(vo_state, number)
+    out_grad_ref[...] = pair_step(out_state, outer - 1)
+    qkv_grad_ref[:, : 2 * heads_wide] = pair_step(qk_state, outer - 1)
+    qkv_grad_ref[:, 2 * heads_wide :] = pair_step(vo_state, outer - 1)
     gain_ref[...] = total(gain_group, gain_copies)
-    qkv_grad_ref[...] = total(qkv_parts, qkv_across)
     for copy, condition in sent:
         if condition is None:
             copy.wait_send()
@@ -1044,6 +1097,7 @@
     pad_hidden = -(-3 * hidden // 128) * 128
     row_count = own_rows * members
     head_count, spread = heads_wide // HD, 2 * heads_wide
+    side = -3 * heads_wide % 128
     outer, rings = groups // 2, members // 2
     vmem = pltpu.VMEM
     parts = vmem((members, own_rows, width), bf16)
@@ -1061,8 +1115,9 @@
         vmem(w_qkv.shape, bf16), vmem(w_out.shape, bf16),
         vmem(w_in.shape, bf16), vmem(w_down.shape, bf16),
         vmem((1, block), bf16), vmem((1, block), bf16), vmem((row_count, 2 * HD), f32),
-        vmem((groups, block, 4 * heads_wide), bf16),
+        vmem((groups, block, 3 * heads_wide + side), bf16),
         vmem((groups, block, pad_hidden), bf16),
+        vmem((groups, block, heads_wide - side), bf16),
         vmem((groups, 16, 128), bf16),
         vmem((16, width), f32),
         vmem((groups, block, 3 * spread), bf16),
@@ -1083,17 +1138,18 @@
         *exchanged(pad_hidden),
         vmem((own_rows, width), f32),
         parts,
-        *exchanged(heads_wide),
+        *exchanged(heads_wide - side),
         vmem((row_count, 3 * heads_wide), bf16),
-        *exchanged(3 * heads_wide),
+        *exchanged(2 * heads_wide),
+        *exchanged(heads_wide + side),
         parts, arrived, passed,
         vmem((groups, 8, 128), f32), vmem((groups, 8, 128), f32), vmem((members, 8, 128), f32),
     ]
     cuts = 2 if block % 32 == 0 else 1
     chains = 2 * cuts * (4 * (outer - 1) + 1)
     halves = 2 if own_rows % 32 == 0 else 1
-    gathers = 2 * outer - 1 + chains + (3 + halves) * (2 * rings - 1)
-    reduces = (3 + halves) * (2 * rings - 1) + 3 * (2 * outer - 1)
+    gathers = 2 * (2 * outer - 1) + chains + (3 + halves) * (2 * rings - 1)
+    reduces = (3 + halves) * (2 * rings - 1) + 4 * (2 * outer - 1)
     slots = gathers + reduces + groups + members - 2
     dims = (own_rows, width, block, heads_wide, hidden, pad_hidden)
     output, input_grad, gains, qkv_sum, out_sum, mlp_sums = pl.pallas_call(
@@ -1102,8 +1158,8 @@
             jax.ShapeDtypeStruct((own_rows, width), bf16),
             jax.ShapeDtypeStruct((own_rows, width), f32),
             jax.ShapeDtypeStruct((8, 128), f32),
-            jax.ShapeDtypeStruct((block, 3 * heads_wide), f32),
-            jax.ShapeDtypeStruct((block, heads_wide), f32),
+            jax.ShapeDtypeStruct((block, 3 * heads_wide + side), f32),
+            jax.ShapeDtypeStruct((block, heads_wide - side), f32),
             jax.ShapeDtypeStruct((block, pad_hidden), f32),
         ],
         in_specs=[pl.BlockSpec(memory_space=pltpu.HBM)] * 9,
@@ -1184,14 +1240,17 @@
     put(attn_buf, attn_to)
     mlp_buf[...] = gains[1:2, : mlp_buf.shape[1]]
     put(mlp_buf, mlp_to)
-    heads_wide = out_sum.shape[1]
+    heads_wide = out_buf.shape[0]
+    side = heads_wide - out_sum.shape[1]
     for which in range(3):
         qkv_buf[which] = qkv_sum[:, which * heads_wide : (which + 1) * heads_wide]
     put(qkv_buf, qkv_to)
     for which in range(2):
         up_buf[which] = mlp_sums[:, which * hidden : (which + 1) * hidden]
     put(up_buf, up_to)
-    out_buf[...] = jnp.transpose(out_sum[...])
+    if side:
+        out_buf[:side] = jnp.transpose(qkv_sum[:, 3 * heads_wide :])
+    out_buf[side:] = jnp.transpose(out_sum[...])
     put(out_buf, out_to)
     down_buf[...] = jnp.transpose(mlp_sums[:, 2 * hidden : 3 * hidden])
     put(down_buf, down_to)
@@ -1203,7 +1262,8 @@
     row_count = tokens.shape[0] * sizes["tensor"]
     even = sizes["dp"] % 2 == 0 and sizes["tensor"] % 2 == 0
     tiled = w_qkv.shape[1] % 16 == 0 and tokens.shape[0] % 16 == 0
-    return even and tiled and row_count == L and w_qkv.shape[1] <= 128
+    narrow = -3 * w_qkv.shape[2] % 128 < w_qkv.shape[2] and w_qkv.shape[1] <= 128
+    return even and tiled and row_count == L and narrow
 
 
 def layer(sizes, tokens, attn_gain, w_qkv, *rest):

time: 86.1 us -> 85.6 us (level)
  no operation moved by 1% of the time
where the time goes in v4:
time: 85.6 us; the launch traced here: 85.5 us
  Pallas kernels  84.6 us (99%)
    pallas_call x1, Pallas kernels, whole_layer(): pl.pallas_call(functools.partial(layer_kernel, sizes, dims), out_shape=[j...  83.5 us

profile of v4, /device:TPU:0, one launch (start us, length us, event | category | flops | bytes accessed | tf_op | source)
XLA Modules:
  0.0 85.5 jit_solution(933209425876593376)
XLA Ops:
  0.6 83.5 %shard_map.152 = (bf16[128,768]{1,0:T(8,128)(2,1)S(1)}, f32[128,768]{1,0:T(8,128)S(1)}, f32[8,128]{1,0:T(8,128)S(1)}, f32[96,640]{1,0:T(8,128)S(1)}, f32[96,128]{1,0:T(8,128)S(1)}, /*index=5*/f32[96,896]{1,0:T(8,128)S(1)}) custom-call(bf16[128,768]{1,0:T(8,128)(2,1)} %refs_0_.1, bf16[128,768]{1,0:T(8,128)(2,1)} %refs_1_.1, bf16[3,96,192]{2,1,0:T(8,128)(2,1)} %refs_2_.1, ...), custom_call_target="tpu_custom_call" | custom-call | tf_op jit(solution)/shard_map/pallas_call | solution.py:1155
  84.1 1.2 %shard_map.153 = (bf16[128,768]{1,0:T(8,128)(2,1)}, f32[128,768]{1,0:T(8,128)}, f32[3,96,192]{2,1,0:T(8,128)}, f32[192,96]{1,0:T(8,128)}, f32[2,96,288]{2,1,0:T(...) custom-call(bf16[128,768]{1,0:T(8,128)(2,1)S(1)} %get-tuple-element.22.refs_0_, ...), custom_call_target="tpu_custom_call" | custom-call | tf_op jit(solution)/shard_map/pallas_call | solution.py:1186

commit v5 on v4

--- a/solution.py
+++ b/solution.py
@@ -746,10 +746,10 @@
     for copy in chain_a.own:
         copy.wait_recv()
     expand(x_peer)
-    chain_b.step(1)
     for number in range(1, outer):
         chain_a.paired(number, expand)
 
+    chain_b.step(1)
     paired = paired_matrix()
     rotary = table[...]
     for which in range(3):
@@ -836,14 +836,14 @@
         far = lax.rem(yrow + shift, rings)
         project(part_one, far, mixed_ring(far), out_weight)
     first_one = [reduce_far(part_one, recv_one, span) for span in spans]
+    for number in range(2, outer - 1):
+        chain_b.step(number)
     project(part_one, yrow, mixed_ring(yrow), out_weight)
     near_one = [reduce_near(part_one, recv_one, span) for span in spans]
     second_one = [
         reduce_middle(part_one, recv_one, fwd_one, first, span)
         for first, span in zip(first_one, spans)
     ]
-    for number in range(2, outer - 1):
-        chain_b.step(number)
     for head in range(head_count):
         q_buf[head] = dot_f32(q_buf[head], paired, 1, 0).astype(bf16)
         k_buf[head] = dot_f32(k_buf[head], paired, 1, 0).astype(bf16)
@@ -1017,6 +1017,8 @@
         .reshape(groups, block, heads_wide)
     )
     vo_pairs = pair_start(vo_grads, vo_half)
+    out_state = (out_grads, out_half, out_sum, out_parts, out_pairs, [])
+    pair_step(out_state, 0)
     qkv_weight = w_a[:, :, : 3 * heads_wide].reshape(width, 3 * heads_wide)
 
     def grad_ring(ring):
@@ -1035,15 +1037,16 @@
             copy.wait_recv()
         return jnp.sum(parts[...].astype(f32), axis=0)
 
-    mlp_out = reduce_finish(part_three, recv_three, near_three, second_three)
-    output_ref[...] = (hidden_res[...] + mlp_out).astype(bf16)
-    out_state = (out_grads, out_half, out_sum, out_parts, out_pairs, [])
-    for number in range(outer - 1):
-        pair_step(out_state, number)
-    mlp_grad_ref[...] = pair_step(mlp_state, outer - 1)
     qk_state = (qk_grads, qk_half, qk_sum, qk_parts, qk_pairs, [])
     vo_state = (vo_grads, vo_half, vo_sum, vo_parts, vo_pairs, [])
     pair_step(qk_state, 0)
+    for number in range(1, outer - 1):
+        pair_step(out_state, number)
+    mlp_out = reduce_finish(part_three, recv_three, near_three, second_three)
+    output_ref[...] = (hidden_res[...] + mlp_out).astype(bf16)
+    mlp_grad_ref[...] = pair_step(mlp_state, outer - 1)
+    for number in range(1, min(2, outer - 1)):
+        pair_step(qk_state, number)
     residual = tok_buf[me_t].astype(f32)
     normed_one, inv_one = normalize(residual)
     back_one = reduce_finish(part_four, recv_four, near_four, second_four)
@@ -1060,16 +1063,15 @@
     for shift in range(1, groups):
         peer = lax.rem(me_d + shift, groups)
         gain_copies.append(send(gain_send.at[peer], gain_recv.at[me_d], "dp", peer))
-    for number in range(1, outer - 1):
+    for number in range(2, outer - 1):
         pair_step(qk_state, number)
-    pair_step(vo_state, 0)
+    for number in range(outer - 1):
+        pair_step(vo_state, number)
     gain_group[me_t] = total(gain_recv, gain_copies)
     gain_copies = []
     for shift in range(1, members):
         peer = lax.rem(me_t + shift, members)
         gain_copies.append(send(gain_group.at[me_t], gain_group.at[me_t], "tensor", peer))
-    for number in range(1, outer - 1):
-        pair_step(vo_state, number)
     out_grad_ref[...] = pair_step(out_state, outer - 1)
     qkv_grad_ref[:, : 2 * heads_wide] = pair_step(qk_state, outer - 1)
     qkv_grad_ref[:, 2 * heads_wide :] = pair_step(vo_state, outer - 1)

time: 85.6 us -> 84.2 us (0.984)
  Pallas kernels: 84.6 us -> 83.2 us
    pallas_call x1, Pallas kernels: 83.5 us -> 82 us  [whole_layer(): pl.pallas_call(functools.partial(layer_kernel, sizes, dims), out_shape=[j...]
where the time goes in v5:
time: 84.2 us; the launch traced here: 84 us
  Pallas kernels  83.2 us (99%)
    pallas_call x1, Pallas kernels, whole_layer(): pl.pallas_call(functools.partial(layer_kernel, sizes, dims), out_shape=[j...  82 us

profile of v5, /device:TPU:0, one launch (start us, length us, event | category | flops | bytes accessed | tf_op | source)
XLA Modules:
  0.0 84.0 jit_solution(2762958049211193040)
XLA Ops:
  0.6 82.0 %shard_map.152 = (bf16[128,768]{1,0:T(8,128)(2,1)S(1)}, f32[128,768]{1,0:T(8,128)S(1)}, f32[8,128]{1,0:T(8,128)S(1)}, f32[96,640]{1,0:T(8,128)S(1)}, f32[96,128]{1,0:T(8,128)S(1)}, /*index=5*/f32[96,896]{1,0:T(8,128)S(1)}) custom-call(bf16[128,768]{1,0:T(8,128)(2,1)} %refs_0_.1, bf16[128,768]{1,0:T(8,128)(2,1)} %refs_1_.1, bf16[3,96,192]{2,1,0:T(8,128)(2,1)} %refs_2_.1, ...), custom_call_target="tpu_custom_call" | custom-call | tf_op jit(solution)/shard_map/pallas_call | solution.py:1157
  82.7 1.2 %shard_map.153 = (bf16[128,768]{1,0:T(8,128)(2,1)}, f32[128,768]{1,0:T(8,128)}, f32[3,96,192]{2,1,0:T(8,128)}, f32[192,96]{1,0:T(8,128)}, f32[2,96,288]{2,1,0:T(...) custom-call(bf16[128,768]{1,0:T(8,128)(2,1)S(1)} %get-tuple-element.22.refs_0_, ...), custom_call_target="tpu_custom_call" | custom-call | tf_op jit(solution)/shard_map/pallas_call | solution.py:1188
